TPU v7x, 32 devices: a whole 2x2x4 slice. The times are simulated.
32 devices in a mesh: seq: 16 (over z, y, x), wa: 2 (over core).
Axes of the slice: x: 2, y: 2, z: 4, core: 2. Of those that a mesh axis runs over, the one named last changes fastest.
Arguments:
- tokens: bfloat16 [2, 5120, 768], P('wa', 'seq'), may hold values from -6 to 6
- cotangent: bfloat16 [2, 5120, 768], P('wa', 'seq'), may hold values from -6 to 6
- w_qkv: bfloat16 [3, 768, 768], P(None, None, 'wa'), may hold values from -0.21875 to 0.21875
- w_out: bfloat16 [768, 768], P('wa'), may hold values from -0.875 to 0.875
- w_up: bfloat16 [768, 3072], P(None, 'wa'), may hold values from -0.21875 to 0.21875
- w_down: bfloat16 [3072, 768], P('wa'), may hold values from -0.109375 to 0.109375
- gain_attn: bfloat16 [768], P('wa'), may hold values from 0.25 to 1.75
- gain_mlp: bfloat16 [768], P('wa'), may hold values from 0.25 to 1.75
- router: bfloat16 [768], P('wa'), may hold values from -0.21875 to 0.21875
- picked: int32 [2, 1280], replicated, may hold values from 0 to 319, as said below
- counts: int32 [2, 16], replicated, may hold values from 1 to 80, as said below
Outputs:
- mixed: bfloat16 [2, 5120, 768], P('wa', 'seq')
- grad_tokens: bfloat16 [2, 5120, 768], P('wa', 'seq')
- grad_qkv: float32 [3, 768, 768], P(None, None, 'wa')
- grad_out: float32 [768, 768], P('wa')
- grad_up: float32 [768, 3072], P(None, 'wa')
- grad_down: float32 [3072, 768], P('wa')
- grad_gain_attn: float32 [768], P('wa')
- grad_gain_mlp: float32 [768], P('wa')
- grad_router: float32 [768], P('wa')
Inputs may be any that keep to these rules, and one draw needn't show every extreme that they name: For stream s and device d, entries d * 80 to d * 80 + counts[s, d] - 1 of picked[s] are the indices of that device's selected tokens within its block; the 80 entries of one device are distinct. `counts`: selected tokens of stream s on device d; in each stream some device has exactly 80.
All inputs are finite; a program needn't handle non-finite values.
Results may differ from a plain program's by a relative error of at most 0.014.
The roundings to bfloat16 on the way count: a program that leaves them out, or rounds other values in their place, can miss the bound.
Values may be sent and summed in bfloat16 or wider, within the bound.
A program may use at most 320 MiB of HBM per device.

v0:
```python
import jax
import jax.numpy as jnp
from jax import lax
from jax.sharding import PartitionSpec as P

HD = 64
CAP = 80


EPS = 1e-05
NEG = -1e30


def norm_rows(value, gain):
    scale = lax.rsqrt(jnp.mean(value * value, axis=-1, keepdims=True) + EPS)
    return (value * scale * gain, scale)


def norm_back(value, scale, gain, grad_out):
    normed = value * scale
    weighted = grad_out * gain
    grad_value = scale * (weighted - normed * jnp.mean(weighted * normed, axis=-1, keepdims=True))
    return (grad_value, normed)


def gelu_back(pre, grad):
    unused, pull = jax.vjp(lambda value: jax.nn.gelu(value, approximate=True), pre)
    return pull(grad)[0]


def body(
    tokens, cotangent, w_qkv, w_out, w_up, w_down, gain_attn, gain_mlp, router, picked, counts
):
    f32 = jnp.float32
    bf16 = jnp.bfloat16
    nseq = lax.axis_size("seq")
    me = lax.axis_index("seq")
    side = lax.axis_index("wa")
    slots = jnp.arange(CAP, dtype=jnp.int32)
    own_rows = lax.dynamic_slice(picked, (side, me * CAP), (1, CAP))[0]
    x_own = jnp.take(tokens[0], own_rows, axis=0)
    dy_own = jnp.take(cotangent[0], own_rows, axis=0).astype(f32)
    x_rows, g_attn, g_mlp, w_router = (
        lax.all_gather(x_own[None], "wa", axis=0, tiled=True),
        lax.all_gather(gain_attn, "wa", axis=0, tiled=True),
        lax.all_gather(gain_mlp, "wa", axis=0, tiled=True),
        lax.all_gather(router, "wa", axis=0, tiled=True),
    )
    qkv_w, out_w, up_w, down_w = (w_qkv, w_out, w_up, w_down)
    streams = jnp.arange(lax.axis_size("wa"))
    stream_picked = jnp.take(picked, streams, axis=0)
    stream_counts = jnp.take(counts, streams, axis=0)
    key_index = jnp.arange(nseq * CAP, dtype=jnp.int32)
    key_device = key_index // CAP
    key_pos = stream_picked * nseq + key_device[None, :]
    key_live = (key_index % CAP)[None, :] < jnp.take(stream_counts, key_device, axis=1)
    query_index = me * CAP + slots
    query_pos = lax.dynamic_slice_in_dim(key_pos, me * CAP, CAP, 1)
    own_live = (slots < counts[side, me]).astype(f32)
    gains_a = g_attn.astype(f32)
    gains_m = g_mlp.astype(f32)
    x_keep = x_own.astype(f32)
    weight = jax.nn.sigmoid(jnp.dot(x_own, w_router, preferred_element_type=f32))
    x_wide = x_rows.astype(f32)
    normed_a, scale_a = norm_rows(x_wide, gains_a)
    u_rows = normed_a.astype(bf16)
    qkv = jnp.einsum("srd,cde->csre", u_rows, qkv_w, preferred_element_type=f32).astype(bf16)
    query = qkv[0]
    local_kv = qkv[1:]
    batch = query.shape[0]
    heads = query.shape[-1] // HD
    factor = HD ** (-0.5)
    split_q = query.reshape(batch, CAP, heads, HD)
    kv_all = lax.all_gather(local_kv, "seq", axis=2, tiled=True)
    block = 8 * CAP
    nblock = kv_all.shape[2] // block

    def block_of(start):
        keys_b = lax.dynamic_slice_in_dim(kv_all[0], start, block, 1).reshape(
            batch, block, heads, HD
        )
        vals_b = lax.dynamic_slice_in_dim(kv_all[1], start, block, 1).reshape(
            batch, block, heads, HD
        )
        k_pos = lax.dynamic_slice_in_dim(key_pos, start, block, 1)
        k_live = lax.dynamic_slice_in_dim(key_live, start, block, 1)
        k_index = start + jnp.arange(block, dtype=jnp.int32)
        allowed = (k_pos[:, None, :] <= query_pos[:, :, None]) & (
            k_live[:, None, :] | (k_index[None, None, :] == query_index[None, :, None])
        )
        raw = jnp.einsum("sqhd,skhd->shqk", split_q, keys_b, preferred_element_type=f32) * factor
        return (keys_b, vals_b, allowed, jnp.where(allowed[:, None], raw, NEG))

    def max_sum(number, carry):
        top, total = carry
        unused_k, unused_v, allowed, scores = block_of(number * block)
        new_top = jnp.maximum(top, jnp.max(scores, axis=-1, keepdims=True))
        expd = jnp.where(allowed[:, None], jnp.exp(scores - new_top), 0.0)
        return (new_top, total * jnp.exp(top - new_top) + jnp.sum(expd, axis=-1, keepdims=True))

    top_start = jnp.full((batch, heads, CAP, 1), NEG, f32)
    top, total = lax.fori_loop(
        0, nblock, max_sum, (top_start, jnp.zeros((batch, heads, CAP, 1), f32))
    )
    lse = top + jnp.log(total)

    def weigh(number, acc):
        unused_k, vals_b, allowed, scores = block_of(number * block)
        probs_low = jnp.exp(scores - lse).astype(bf16)
        return acc + jnp.einsum("shqk,skhd->sqhd", probs_low, vals_b, preferred_element_type=f32)

    acc = lax.fori_loop(0, nblock, weigh, jnp.zeros((batch, CAP, heads, HD), f32))
    attended = acc.reshape(query.shape).astype(bf16)
    attn_part = jnp.einsum("sqe,ed->sqd", attended, out_w, preferred_element_type=f32)
    attn_own = lax.psum_scatter(attn_part, "wa", scatter_dimension=0, tiled=True)[0]
    resid = x_keep + attn_own
    normed_m, scale_m = norm_rows(resid, gains_m)
    w_own = normed_m.astype(bf16)
    w_rows = lax.all_gather(w_own[None], "wa", axis=0, tiled=True)
    pre = jnp.einsum("srd,df->srf", w_rows, up_w, preferred_element_type=f32)
    act = jax.nn.gelu(pre, approximate=True).astype(bf16)
    mlp_part = jnp.einsum("srf,fd->srd", act, down_w, preferred_element_type=f32)
    mlp_own = lax.psum_scatter(
        mlp_part.astype(jnp.bfloat16), "wa", scatter_dimension=0, tiled=True
    ).astype(jnp.float32)[0]
    branch = attn_own + mlp_own
    lift = (weight * own_live)[:, None]
    out_rows = (x_keep + lift * branch).astype(bf16)
    mixed_out = tokens.at[0, own_rows].set(out_rows)
    grad_branch = dy_own * lift
    grad_logit = jnp.sum(dy_own * branch, axis=-1) * own_live * weight * (1.0 - weight)
    grad_router = jnp.dot(grad_logit, x_keep, precision=lax.Precision.HIGHEST)
    grad_m = grad_branch.astype(bf16)
    grad_m_rows = lax.all_gather(grad_m[None], "wa", axis=0, tiled=True)
    grad_down = jnp.einsum("srf,srd->fd", act, grad_m_rows, preferred_element_type=f32)
    grad_act = jnp.einsum("srd,fd->srf", grad_m_rows, down_w, preferred_element_type=f32)
    grad_pre = gelu_back(pre, grad_act).astype(bf16)
    grad_up = jnp.einsum("srd,srf->df", w_rows, grad_pre, preferred_element_type=f32)
    grad_w_part = jnp.einsum("srf,df->srd", grad_pre, up_w, preferred_element_type=f32)
    grad_w_own = lax.psum_scatter(grad_w_part, "wa", scatter_dimension=0, tiled=True)[0]
    grad_resid, hat_m = norm_back(resid, scale_m, gains_m, grad_w_own)
    grad_gain_m = jnp.sum(grad_w_own * hat_m, axis=0)
    grad_a = (grad_branch + grad_resid).astype(bf16)
    grad_a_rows = lax.all_gather(grad_a[None], "wa", axis=0, tiled=True)
    grad_out = jnp.einsum("sqe,sqd->ed", attended, grad_a_rows, preferred_element_type=f32)
    grad_attended = jnp.einsum(
        "sqd,ed->sqe", grad_a_rows, out_w, preferred_element_type=f32
    ).astype(bf16)
    split_do = grad_attended.reshape(batch, CAP, heads, HD)

    def delta_step(number, delta):
        unused_k, vals_b, allowed, scores = block_of(number * block)
        probs = jnp.exp(scores - lse)
        grad_probs = jnp.einsum("sqhd,skhd->shqk", split_do, vals_b, preferred_element_type=f32)
        return delta + jnp.sum(grad_probs * probs, axis=-1, keepdims=True)

    delta = lax.fori_loop(0, nblock, delta_step, jnp.zeros((batch, heads, CAP, 1), f32))

    def grad_step(number, carry):
        grad_query, holder = carry
        start = number * block
        keys_b, vals_b, allowed, scores = block_of(start)
        probs = jnp.exp(scores - lse)
        grad_probs = jnp.einsum("sqhd,skhd->shqk", split_do, vals_b, preferred_element_type=f32)
        grad_scores = (probs * (grad_probs - delta)).astype(bf16)
        grad_query = (
            grad_query
            + jnp.einsum("shqk,skhd->sqhd", grad_scores, keys_b, preferred_element_type=f32)
            * factor
        )
        grad_keys = (
            jnp.einsum("shqk,sqhd->skhd", grad_scores, split_q, preferred_element_type=f32) * factor
        )
        grad_values = jnp.einsum(
            "shqk,sqhd->skhd", probs.astype(bf16), split_do, preferred_element_type=f32
        )
        paired = jnp.stack([grad_keys, grad_values]).reshape(2, batch, block, heads * HD)
        holder = lax.dynamic_update_slice_in_dim(holder, paired, start, 2)
        return (grad_query, holder)

    grad_query, holder = lax.fori_loop(
        0,
        nblock,
        grad_step,
        (jnp.zeros((batch, CAP, heads, HD), f32), jnp.zeros(kv_all.shape, f32)),
    )
    kv_total = lax.psum_scatter(holder, "seq", scatter_dimension=2, tiled=True)
    grad_qkv_rows = jnp.concatenate(
        [grad_query.reshape(query.shape)[None].astype(bf16), kv_total.astype(bf16)], axis=0
    )
    grad_qkv = jnp.einsum("srd,csre->cde", u_rows, grad_qkv_rows, preferred_element_type=f32)
    grad_u_part = jnp.einsum("csre,cde->srd", grad_qkv_rows, qkv_w, preferred_element_type=f32)
    part_gain_a = jnp.sum(grad_u_part * (x_wide * scale_a), axis=(0, 1))
    grad_u_all, grad_gain_a, grad_gain_m, grad_router = (
        lax.psum_scatter(
            grad_u_part.astype(jnp.bfloat16), "wa", scatter_dimension=0, tiled=True
        ).astype(jnp.float32),
        lax.psum_scatter(
            part_gain_a.astype(jnp.bfloat16), "wa", scatter_dimension=0, tiled=True
        ).astype(jnp.float32),
        lax.psum_scatter(
            grad_gain_m.astype(jnp.bfloat16), "wa", scatter_dimension=0, tiled=True
        ).astype(jnp.float32),
        lax.psum_scatter(
            grad_router.astype(jnp.bfloat16), "wa", scatter_dimension=0, tiled=True
        ).astype(jnp.float32),
    )
    grad_u_own = grad_u_all[0]
    grad_x_norm, unused = norm_back(x_keep, scale_a[side], gains_a, grad_u_own)
    grad_rows = grad_x_norm + grad_resid + grad_logit[:, None] * w_router.astype(f32)[None, :]
    grad_tokens = cotangent.astype(f32).at[0, own_rows].add(grad_rows).astype(bf16)
    shares = (grad_qkv, grad_out, grad_up, grad_down, grad_gain_a, grad_gain_m, grad_router)
    summed = lax.psum(
        (shares[0], shares[1], shares[2], shares[3], shares[4], shares[5], shares[6]), "seq"
    )
    return (
        mixed_out,
        grad_tokens,
        summed[0],
        summed[1],
        summed[2],
        summed[3],
        summed[4],
        summed[5],
        summed[6],
    )


def solution(mesh):
    return jax.shard_map(
        body,
        mesh=mesh,
        in_specs=(
            P("wa", "seq", None),
            P("wa", "seq", None),
            P(None, None, "wa"),
            P("wa", None),
            P(None, "wa"),
            P("wa", None),
            P("wa"),
            P("wa"),
            P("wa"),
            P(),
            P(),
        ),
        out_specs=(
            P("wa", "seq", None),
            P("wa", "seq", None),
            P(None, None, "wa"),
            P("wa", None),
            P(None, "wa"),
            P("wa", None),
            P("wa"),
            P("wa"),
            P("wa"),
        ),
        check_vma=False,
    )
```

profile of v0, /device:TPU:0, one launch (start us, length us, event | category | flops | bytes accessed | tf_op | source)
XLA Modules:
  0.0 852.4 jit_solution(13381343570804073223)
XLA Ops:
  10.7 2.1 all-gather
  12.8 1.8 all-gather.5
  15.4 2.0 fusion.57
  21.3 3.2 gather_fusion.2
  24.5 1.9 fusion.76
  27.7 68.0 %all-gather.9.cloned.1.call-done = bf16[2,2,1280,384]{3,2,0,1:T(8,128)(2,1)} async-done(((bf16[2,2,80,384]{3,2,0,1:T(8,128)(2,1)}), bf16[2,2,1280,384]{3,2,0,1:T(8,128)(2,1)}) %all-gather.9.cloned.1.call-update) | async-done | bytes 3932176 | tf_op jit(solution)/shard_map/all_gather | solution.py:74
  95.6 6.3 copy.65
  101.9 14.6 %while.60 = (s32[]{:T(128)}, f32[2,6,80,1]{2,1,0,3:T(8,128)S(1)}, f32[2,6,80,1]{2,1,0,3:T(8,128)S(1)}, s32[2,1280]{1,0:T(2,128)S(1)}, s32[2,80]{1,0:T(2,128)S(1)...) while((s32[]{:T(128)}, f32[2,6,80,1]{2,1,0,3:T(8,128)S(1)}, ...), condition=%wide.region_4.6_spmd.clone, body=%wide.region_1.0_spmd.clone.sunk | while | flops 83922328 | bytes 12404690 | solution.py:102
  102.8 1.7 slice.93
  104.6 2.0 fusion.196
  106.6 2.5 select_reduce_fusion.2
  110.1 1.7 slice.93
  111.9 2.0 fusion.196
  114.0 2.5 select_reduce_fusion.2
  117.1 23.4 %while.61 = (s32[]{:T(128)}, f32[2,80,6,64]{1,3,2,0:T(8,128)}, bf16[2,2,1280,384]{2,3,1,0:T(8,128)(2,1)}, s32[2,1280]{1,0:T(2,128)S(1)}, s32[2,80]{1,0:T(2,128)S...) while((s32[]{:T(128)}, f32[2,80,6,64]{1,3,2,0:T(8,128)}, ...), condition=%wide.region_6.8_spmd.clone, body=%wide.region_5.7_spmd.clone.sunk | while | flops 160226000 | bytes 14713809 | solution.py:112
  117.1 4.3 fusion.200
  121.4 2.6 constant_dynamic-slice_fusion.31
  125.6 3.2 fusion.201
  128.7 4.3 fusion.200
  133.0 2.6 constant_dynamic-slice_fusion.31
  137.2 3.3 fusion.201
  142.3 2.2 fusion.78
  145.3 1.8 all-gather.6
  149.9 1.8 all-gather.4
  153.1 2.1 all-gather.2
  157.5 2.0 all-gather.1
  159.4 2.3 fusion.45
  162.7 1.4 fusion.60
  164.2 2.6 fusion.73
  166.9 1.7 fusion.43
  168.7 1.8 reduce-scatter.8.cloned.1.call-done
  170.5 11.8 %reduce-scatter.10.cloned.1.call-done = f32[1,80,768]{2,1,0:T(8,128)} async-done(((f32[2,80,768]{2,1,0:T(8,128)}), f32[1,80,768]{2,1,0:T(8,128)}) %reduce-scatter.10.cloned.1.call-update) | async-done | bytes 245776 | tf_op jit(solution)/shard_map/reduce_scatter | solution.py:140
  184.8 2.2 all-gather.3
  187.7 15.4 %while.62 = (s32[]{:T(128)}, f32[2,6,80,1]{2,0,1,3:T(2,128)S(1)}, bf16[2,2,1280,384]{2,3,1,0:T(8,128)(2,1)}, bf16[2,80,6,64]{1,3,2,0:T(8,128)(2,1)S(1)}, s32[2,1...) while((s32[]{:T(128)}, f32[2,6,80,1]{2,0,1,3:T(2,128)S(1)}, ...), condition=%wide.region_15.17_spmd.clone, body=%wide.region_13.16_spmd.clone.sunk | while | flops 160718496 | bytes 19275736 | solution.py:157
  187.7 3.7 fusion.206
  191.3 1.4 constant_dynamic-slice_fusion.34
  195.3 3.7 fusion.206
  199.0 1.4 constant_dynamic-slice_fusion.34
  203.1 3.6 broadcast_in_dim.274.clone
  206.7 49.0 %while.63 = (s32[]{:T(128)}, f32[2,80,6,64]{1,3,2,0:T(8,128)S(1)}, f32[2,2,1280,384]{3,2,0,1:T(8,128)}, bf16[2,2,1280,384]{2,3,1,0:T(8,128)(2,1)}, s32[2,1280]{1...) while((s32[]{:T(128)}, f32[2,80,6,64]{1,3,2,0:T(8,128)S(1)}, ...), condition=%wide.region_17.19_spmd.clone, body=%wide.region_16.18_spmd.clone.sunk | while | flops 401378016 | bytes 84251224 | solution.py:181
  206.7 4.3 fusion.219
  211.0 1.7 constant_dynamic-slice_fusion.37
  219.1 2.2 pad_maximum_fusion.5
  221.3 5.6 copy.95
  226.9 4.3 constant_dynamic-update-slice_fusion.2
  231.2 4.3 fusion.219
  235.5 1.7 constant_dynamic-slice_fusion.37
  243.6 2.2 pad_maximum_fusion.5
  245.8 5.6 copy.95
  251.5 4.2 constant_dynamic-update-slice_fusion.2
  257.0 3.2 convolution_bitcast_fusion
  260.4 152.4 %reduce-scatter.12.cloned.1.call-done = f32[2,2,80,384]{3,2,0,1:T(8,128)} async-done(((f32[2,2,1280,384]{3,2,0,1:T(8,128)}), f32[2,2,80,384]{3,2,0,1:T(8,128)}) %reduce-scatter.12.cloned.1.call-update) | async-done | bytes 491536 | tf_op jit(solution)/shard_map/reduce_scatter | solution.py:187
  413.8 2.9 fusion.83
  416.8 3.0 convolution_bitcast_fusion.1
  419.8 1.4 convolution_bitcast_fusion.3
  421.2 2.5 convolution_bitcast_fusion.2
  426.6 1.3 scatter_custom_fusion
  428.8 2.5 all-reduce.6
  431.5 43.5 %all-reduce.4 = (f32[384]{0:T(512)}, f32[384]{0:T(512)}, f32[384]{0:T(512)}) all-reduce(f32[384]{0:T(512)S(1)} %dynamic-slice_convert_fusion.2, f32[384]{0:T(512)S(1)} %get-tuple-element.1100, f32[384]{0:T(512)S(1)} %get-tuple-element.1099), channel_id=1, replica_groups=mesh['seq'=16,'wa'=2] {'seq'}, use_global_device_ids=true, to_apply=%region_29.31 | all-reduce | flops 1152 | bytes 9216 | tf_op jit(solution)/shard_map/psum | solution.py:213
  476.2 2.1 scatter_custom_fusion.1
  479.2 352.4 %all-reduce.9.cloned.1.call-done = (f32[3,768,384]{1,2,0:T(8,128)}, f32[384,768]{1,0:T(8,128)}, f32[768,1536]{1,0:T(8,128)}, f32[1536,768]{1,0:T(8,128)}) async-done(((f32[3,768,384]{1,2,0:T(8,128)}, f32[384,768]{1,0:T(8,128)}, f32[768,1536]{1,0:T(8,128)}, f32[1536,768]{1,0:T(8,128)}), (f32[3,768,384]{1,2,0:T(8,128)}, f32[384,768]{1,0:T(8,128)}, f32[768,1536]{1,0:T(8,128)}, ...) | async-done | bytes 14155792 | tf_op jit(solution)/shard_map/psum | solution.py:213
  831.5 5.2 copy.77
  837.8 5.5 copy.136
  843.3 2.2 copy.137
  (287 shorter events, 54.7 us)
Async XLA Ops:
  7.2 155.5 %copy-start = (bf16[1536,768]{1,0:T(8,128)(2,1)S(1)}, bf16[1536,768]{1,0:T(8,128)(2,1)}, u32[]{:S(2)}) copy-start(bf16[1536,768]{1,0:T(8,128)(2,1)} %param.26) | copy-start | bytes 7077892
  7.2 5.6 copy-start.55
  7.2 88.4 %all-gather.9.cloned.1.call-start = ((), (), s32[]{:S(2)}) async-start(), calls=%async_computation.5 | async-start | bytes 4177920 | tf_op jit(solution)/shard_map/all_gather | solution.py:74
  8.4 10.5 %copy-start.12 = (bf16[1,320,768]{2,1,0:T(8,128)(2,1)}, bf16[1,320,768]{2,1,0:T(8,128)(2,1)S(1)}, u32[]{:S(2)}) copy-start(bf16[1,320,768]{2,1,0:T(8,128)(2,1)S(1)} %copy.134) | copy-start | bytes 1474564
  9.2 5.4 copy-start.43
  9.2 0.8 copy-start.52
  9.2 10.7 %copy-start.37 = (s32[2,1280]{1,0:T(2,128)S(1)}, s32[2,1280]{1,0:T(2,128)}, u32[]{:S(2)}) copy-start(s32[2,1280]{1,0:T(2,128)} %param.30) | copy-start | bytes 30724
  10.0 16.5 %copy-start.6 = (bf16[80,768]{1,0:T(8,128)(2,1)}, bf16[80,768]{1,0:T(8,128)(2,1)S(1)}, u32[]{:S(2)}) copy-start(bf16[80,768]{1,0:T(8,128)(2,1)S(1)} %gather_fusion.3) | copy-start | bytes 368644
  10.0 10.6 %copy-start.42 = (s32[2,16]{1,0:T(2,128)S(1)}, s32[2,16]{1,0:T(2,128)}, u32[]{:S(2)}) copy-start(s32[2,16]{1,0:T(2,128)} %param.31) | copy-start | bytes 388
  12.8 14.5 %copy-start.17 = (bf16[160,768]{1,0:T(8,128)(2,1)}, bf16[160,768]{1,0:T(8,128)(2,1)S(1)}, u32[]{:S(2)}) copy-start(bf16[160,768]{1,0:T(8,128)(2,1)S(1)} %all-gather) | copy-start | bytes 737284
  14.7 12.8 %copy-start.40 = (f32[768]{0:T(1024)}, f32[768]{0:T(1024)S(1)}, u32[]{:S(2)}) copy-start(f32[768]{0:T(1024)S(1)} %reshape.509) | copy-start | bytes 9220
  18.9 136.3 %reduce-scatter.6.cloned.1.call-start = ((), (), s32[]{:S(2)}) async-start(), calls=%async_computation.6 | async-start | bytes 737280 | tf_op jit(solution)/shard_map/reduce_scatter | solution.py:115
  140.5 8.5 copy-start.10
  140.5 11.1 %copy-start.34 = (bf16[80,768]{1,0:T(8,128)(2,1)S(1)}, bf16[80,768]{1,0:T(8,128)(2,1)}, u32[]{:S(2)}) copy-start(bf16[80,768]{1,0:T(8,128)(2,1)} %copy-done.33) | copy-start | bytes 368644
  140.5 12.5 %copy-start.44 = (pred[80]{0:T(512)(128)(4,1)S(1)}, pred[80]{0:T(512)(128)(4,1)}, u32[]{:S(2)}) copy-start(pred[80]{0:T(512)(128)(4,1)} %copy-done.43) | copy-start | bytes 244
  140.5 14.7 %copy-start.7 = (bf16[80,768]{1,0:T(8,128)(2,1)S(1)}, bf16[80,768]{1,0:T(8,128)(2,1)}, u32[]{:S(2)}) copy-start(bf16[80,768]{1,0:T(8,128)(2,1)} %copy-done.6) | copy-start | bytes 368644
  144.5 26.0 %reduce-scatter.8.cloned.1.call-start = ((), (), s32[]{:S(2)}) async-start(), calls=%async_computation.7 | async-start | bytes 368640 | tf_op jit(solution)/shard_map/reduce_scatter | solution.py:123
  149.9 11.9 %copy-start.27 = (bf16[80,768]{1,0:T(8,128)(2,1)}, bf16[80,768]{1,0:T(8,128)(2,1)S(1)}, u32[]{:S(2)}) copy-start(bf16[80,768]{1,0:T(8,128)(2,1)S(1)} %gather_fusion.4) | copy-start | bytes 368644
  151.7 10.1 %copy-start.48 = (bf16[2,1,384]{2,1,0:T(2,128)(2,1)}, bf16[2,1,384]{2,1,0:T(2,128)(2,1)S(1)}, u32[]{:S(2)}) copy-start(bf16[2,1,384]{2,1,0:T(2,128)(2,1)S(1)} %all-gather.4) | copy-start | bytes 4612
  153.0 2.2 copy-start.53
  156.4 27.3 %copy-start.50 = (f32[80]{0:T(128)}, f32[80]{0:T(128)S(1)}, u32[]{:S(2)}) copy-start(f32[80]{0:T(128)S(1)} %add_rsqrt_fusion.1) | copy-start | bytes 964
  159.4 4.7 copy-start.19
  161.8 0.9 copy-start.15
  164.2 18.2 %reduce-scatter.10.cloned.1.call-start = ((), (), s32[]{:S(2)}) async-start(), calls=%async_computation.8 | async-start | bytes 737280 | tf_op jit(solution)/shard_map/reduce_scatter | solution.py:140
  164.2 2.7 copy-start.8
  166.9 1.8 copy-start.25
  166.9 15.5 %copy-start.9 = (f32[1,80,768]{2,1,0:T(8,128)S(1)}, f32[1,80,768]{2,1,0:T(8,128)}, u32[]{:S(2)}) copy-start(f32[1,80,768]{2,1,0:T(8,128)} %reduce-scatter.6.cloned.1.call-done) | copy-start | bytes 737284
  166.9 15.4 %copy-start.28 = (bf16[80,768]{1,0:T(8,128)(2,1)S(1)}, bf16[80,768]{1,0:T(8,128)(2,1)}, u32[]{:S(2)}) copy-start(bf16[80,768]{1,0:T(8,128)(2,1)} %copy-done.27) | copy-start | bytes 368644
  166.9 16.8 %copy-start.54 = (f32[80]{0:T(128)S(1)}, f32[80]{0:T(128)}, u32[]{:S(2)}) copy-start(f32[80]{0:T(128)} %copy-done.53) | copy-start | bytes 964
  166.9 20.1 %copy-start.21 = (bf16[384,768]{1,0:T(8,128)(2,1)S(1)}, bf16[384,768]{1,0:T(8,128)(2,1)}, u32[]{:S(2)}) copy-start(bf16[384,768]{1,0:T(8,128)(2,1)} %param.24) | copy-start | bytes 1769476
  168.6 18.9 %copy-start.39 = (f32[2,6,80,1]{2,1,0,3:T(8,128)S(1)}, f32[2,6,80,1]{2,1,0,3:T(8,128)}, u32[]{:S(2)}) copy-start(f32[2,6,80,1]{2,1,0,3:T(8,128)} %get-tuple-element.1601) | copy-start | bytes 11524
  168.6 244.1 %reduce-scatter.12.cloned.1.call-start = ((), (), s32[]{:S(2)}) async-start(), calls=%async_computation.9 | async-start | bytes 8355840 | tf_op jit(solution)/shard_map/reduce_scatter | solution.py:187
  213.2 2.0 copy-start.2
  215.2 1.0 copy-start.4
  215.2 2.1 copy-start.3
  217.4 1.3 copy-start.5
  237.7 2.0 copy-start.2
  239.7 1.0 copy-start.4
  239.8 2.1 copy-start.3
  241.9 1.3 copy-start.5
  255.7 1.2 copy-start.16
  255.7 1.2 copy-start.36
  255.8 158.1 %copy-start.18 = (bf16[160,768]{1,0:T(8,128)(2,1)S(1)}, bf16[160,768]{1,0:T(8,128)(2,1)}, u32[]{:S(2)}) copy-start(bf16[160,768]{1,0:T(8,128)(2,1)} %copy-done.17) | copy-start | bytes 737284
  255.8 158.1 %copy-start.47 = (f32[2,80]{1,0:T(2,128)S(1)}, f32[2,80]{1,0:T(2,128)}, u32[]{:S(2)}) copy-start(f32[2,80]{1,0:T(2,128)} %copy-done.46) | copy-start | bytes 1924
  255.8 219.3 %reduce-scatter.14.cloned.1.call-start = ((), (), s32[]{:S(2)}) async-start(), calls=%async_computation.10 | async-start | bytes 368640 | tf_op jit(solution)/shard_map/reduce_scatter | solution.py:195
  260.2 156.6 %copy-start.20 = (bf16[160,768]{1,0:T(8,128)(2,1)S(1)}, bf16[160,768]{1,0:T(8,128)(2,1)}, u32[]{:S(2)}) copy-start(bf16[160,768]{1,0:T(8,128)(2,1)} %copy-done.19) | copy-start | bytes 737284
  260.2 156.6 %copy-start.26 = (bf16[2,80,1536]{2,1,0:T(8,128)(2,1)S(1)}, bf16[2,80,1536]{2,1,0:T(8,128)(2,1)}, u32[]{:S(2)}) copy-start(bf16[2,80,1536]{2,1,0:T(8,128)(2,1)} %copy-done.25) | copy-start | bytes 1474564
  416.7 3.1 copy-start.23
  416.7 3.1 copy-start.30
  416.7 4.5 copy-start.41
  416.8 414.8 %all-reduce.9.cloned.1.call-start = ((), (), s32[]{:S(2)}) async-start(), calls=%async_computation.11 | async-start | bytes 28311552 | tf_op jit(solution)/shard_map/psum | solution.py:213
  423.7 2.8 copy-start.11
  423.7 2.8 copy-start.13
  423.7 2.8 copy-start.38
  423.8 2.8 copy-start.45
  423.8 4.1 copy-start.56
  423.8 4.8 copy-start.35
  423.8 52.4 %copy-start.24 = (f32[1,80,768]{2,1,0:T(8,128)S(1)}, f32[1,80,768]{2,1,0:T(8,128)}, u32[]{:S(2)}) copy-start(f32[1,80,768]{2,1,0:T(8,128)} %reduce-scatter.10.cloned.1.call-done) | copy-start | bytes 737284
  423.8 52.4 %copy-start.51 = (f32[80]{0:T(128)S(1)}, f32[80]{0:T(128)}, u32[]{:S(2)}) copy-start(f32[80]{0:T(128)} %copy-done.50) | copy-start | bytes 964
  427.9 408.9 %copy-start.14 = (bf16[320,768]{1,0:T(8,128)(2,1)}, bf16[320,768]{1,0:T(8,128)(2,1)S(1)}, u32[]{:S(2)}) copy-start(bf16[320,768]{1,0:T(8,128)(2,1)S(1)} %scatter_custom_fusion) | copy-start | bytes 1474564
  831.5 5.3 copy-start.32
  836.8 6.5 slice-start
  837.8 5.5 slice-start.1
  837.8 7.7 copy-start.1
  (7 other events, 4.7 us)
Sparse Core Ops, SparseCore 0:
  19.1 76.5 all-gather.8
  144.6 6.4 reduce-scatter.5
  164.3 6.2 reduce-scatter.7
  173.2 9.0 reduce-scatter.9
  255.9 156.8 reduce-scatter.11
  416.8 6.9 reduce-scatter.13
  432.0 399.4 all-reduce.8
where the time goes:
time: 854 us; the launch traced here: 852 us
  waiting for transfers between devices  586 us (69%)
  local copies, waits for them, and re-layouts  112 us (13%)
  blocking collectives  59.7 us (7%)
  matrix products  47.3 us (6%)
  other arithmetic  30.5 us (4%)
  between operations  15.6 us (2%)
    psum x1, waiting for transfers between devices, body(): lax.psum((shares[0], shares[1], shares[2], shares[3], shares[4], shares[5...  352 us
    reduce_scatter x1, waiting for transfers between devices, body(): kv_total = lax.psum_scatter(holder, 'seq', scatter_dimension=2, tiled=True)  152 us
    all_gather x1, waiting for transfers between devices, body(): kv_all = lax.all_gather(local_kv, 'seq', axis=2, tiled=True)  68 us
    psum x1, blocking collectives, body(): lax.psum((shares[0], shares[1], shares[2], shares[3], shares[4], shares[5...  43.5 us
    unnamed x125, local copies, waits for them, and re-layouts  29.8 us
    dynamic_update_slice x4, local copies, waits for them, and re-layouts, grad_step(): holder = lax.dynamic_update_slice_in_dim(holder, paired, start, 2)  19.8 us
    slice x6, local copies, waits for them, and re-layouts, block_of(): kv_all[0]  19.3 us
  transfers between devices with their start and end apart: 7, of which 5 were waited for; matrix products, arithmetic and copies ran while one was open for 4% of the time, Pallas kernels for 0%

commit v1 on v0

--- a/solution.py
+++ b/solution.py
@@ -184,7 +184,7 @@
         grad_step,
         (jnp.zeros((batch, CAP, heads, HD), f32), jnp.zeros(kv_all.shape, f32)),
     )
-    kv_total = lax.psum_scatter(holder, "seq", scatter_dimension=2, tiled=True)
+    kv_total = lax.psum_scatter(holder.astype(bf16), "seq", scatter_dimension=2, tiled=True)
     grad_qkv_rows = jnp.concatenate(
         [grad_query.reshape(query.shape)[None].astype(bf16), kv_total.astype(bf16)], axis=0
     )
@@ -210,9 +210,9 @@
     grad_rows = grad_x_norm + grad_resid + grad_logit[:, None] * w_router.astype(f32)[None, :]
     grad_tokens = cotangent.astype(f32).at[0, own_rows].add(grad_rows).astype(bf16)
     shares = (grad_qkv, grad_out, grad_up, grad_down, grad_gain_a, grad_gain_m, grad_router)
-    summed = lax.psum(
-        (shares[0], shares[1], shares[2], shares[3], shares[4], shares[5], shares[6]), "seq"
-    )
+    large = lax.psum(tuple(share.astype(bf16) for share in shares[:4]), "seq")
+    small = lax.psum(shares[4:], "seq")
+    summed = tuple(part.astype(f32) for part in large) + small
     return (
         mixed_out,
         grad_tokens,

time: 854 us -> 645 us (0.76)
  waiting for transfers between devices: 586 us -> 397 us
  local copies, waits for them, and re-layouts: 112 us -> 88.5 us
    psum x1, waiting for transfers between devices: 352 us -> 187 us  [body(): large = lax.psum(tuple((share.astype(bf16) for share in shares[:4])), 'seq')]
    reduce_scatter x1, waiting for transfers between devices: 152 us -> 128 us  [body(): lax.psum_scatter(holder.astype(bf16), 'seq', scatter_dimension=2, tiled=T...]
    dynamic_update_slice x4, local copies, waits for them, and re-layouts: 19.8 us -> 8.63 us  [grad_step(): holder = lax.dynamic_update_slice_in_dim(holder, paired, start, 2)]
    unnamed x125 -> x132, local copies, waits for them, and re-layouts: 29.8 us -> 19.9 us
  transfers between devices with their start and end apart: 7 -> 7, of which waited for: 5 -> 5; matrix products, arithmetic and copies ran while one was open for 4% -> 5% of each run, Pallas kernels for 0% -> 0%
where the time goes in v1:
time: 645 us; the launch traced here: 643 us
  waiting for transfers between devices  397 us (62%)
  local copies, waits for them, and re-layouts  88.5 us (14%)
  blocking collectives  59.5 us (9%)
  matrix products  44.7 us (7%)
  other arithmetic  37.5 us (6%)
  between operations  15.6 us (2%)
    psum x1, waiting for transfers between devices, body(): large = lax.psum(tuple((share.astype(bf16) for share in shares[:4])), 'seq')  187 us
    reduce_scatter x1, waiting for transfers between devices, body(): lax.psum_scatter(holder.astype(bf16), 'seq', scatter_dimension=2, tiled=T...  128 us
    all_gather x1, waiting for transfers between devices, body(): kv_all = lax.all_gather(local_kv, 'seq', axis=2, tiled=True)  68 us
    psum x1, blocking collectives, body(): small = lax.psum(shares[4:], 'seq')  43.3 us
    unnamed x132, local copies, waits for them, and re-layouts  19.9 us
    slice x6, local copies, waits for them, and re-layouts, block_of(): kv_all[0]  19.3 us
  transfers between devices with their start and end apart: 7, of which 5 were waited for; matrix products, arithmetic and copies ran while one was open for 5% of the time, Pallas kernels for 0%

profile of v1, /device:TPU:0, one launch (start us, length us, event | category | flops | bytes accessed | tf_op | source)
XLA Modules:
  0.0 643.2 jit_solution(9726516830229339342)
XLA Ops:
  10.8 2.1 all-gather
  12.8 1.8 all-gather.5
  15.4 2.0 fusion.59
  21.3 3.2 gather_fusion.2
  24.5 1.9 fusion.78
  27.7 68.0 %all-gather.9.cloned.1.call-done = bf16[2,2,1280,384]{3,2,0,1:T(8,128)(2,1)} async-done(((bf16[2,2,80,384]{3,2,0,1:T(8,128)(2,1)}), bf16[2,2,1280,384]{3,2,0,1:T(8,128)(2,1)}) %all-gather.9.cloned.1.call-update) | async-done | bytes 3932176 | tf_op jit(solution)/shard_map/all_gather | solution.py:74
  95.6 6.3 copy.65
  101.9 14.6 %while.60 = (s32[]{:T(128)}, f32[2,6,80,1]{2,1,0,3:T(8,128)S(1)}, f32[2,6,80,1]{2,1,0,3:T(8,128)S(1)}, s32[2,1280]{1,0:T(2,128)S(1)}, s32[2,80]{1,0:T(2,128)S(1)...) while((s32[]{:T(128)}, f32[2,6,80,1]{2,1,0,3:T(8,128)S(1)}, ...), condition=%wide.region_4.6_spmd.clone, body=%wide.region_1.0_spmd.clone.sunk | while | flops 83922328 | bytes 12404690 | solution.py:102
  102.8 1.7 slice.93
  104.6 2.0 fusion.198
  106.7 2.5 select_reduce_fusion.2
  110.2 1.7 slice.93
  111.9 2.0 fusion.198
  114.0 2.5 select_reduce_fusion.2
  117.1 23.4 %while.61 = (s32[]{:T(128)}, f32[2,80,6,64]{1,3,2,0:T(8,128)}, bf16[2,2,1280,384]{2,3,1,0:T(8,128)(2,1)}, s32[2,1280]{1,0:T(2,128)S(1)}, s32[2,80]{1,0:T(2,128)S...) while((s32[]{:T(128)}, f32[2,80,6,64]{1,3,2,0:T(8,128)}, ...), condition=%wide.region_6.8_spmd.clone, body=%wide.region_5.7_spmd.clone.sunk | while | flops 160226000 | bytes 14713809 | solution.py:112
  117.1 4.3 fusion.202
  121.4 2.6 constant_dynamic-slice_fusion.31
  125.6 3.2 fusion.203
  128.8 4.3 fusion.202
  133.1 2.6 constant_dynamic-slice_fusion.31
  137.3 3.3 fusion.203
  142.3 2.2 fusion.80
  145.3 1.8 all-gather.6
  149.9 1.8 all-gather.4
  151.7 1.4 compare_select_fusion.5
  153.2 2.1 all-gather.2
  157.5 2.0 all-gather.1
  159.5 2.3 fusion.45
  162.8 1.4 fusion.62
  164.3 2.6 fusion.75
  167.0 1.7 fusion.43
  168.8 1.8 reduce-scatter.8.cloned.1.call-done
  170.6 11.8 %reduce-scatter.10.cloned.1.call-done = f32[1,80,768]{2,1,0:T(8,128)} async-done(((f32[2,80,768]{2,1,0:T(8,128)}), f32[1,80,768]{2,1,0:T(8,128)}) %reduce-scatter.10.cloned.1.call-update) | async-done | bytes 245776 | tf_op jit(solution)/shard_map/reduce_scatter | solution.py:140
  182.4 1.9 fusion.102
  185.4 2.2 all-gather.3
  188.3 15.5 %while.62 = (s32[]{:T(128)}, f32[2,6,80,1]{2,0,1,3:T(2,128)S(1)}, bf16[2,2,1280,384]{2,3,1,0:T(8,128)(2,1)}, bf16[2,80,6,64]{1,3,2,0:T(8,128)(2,1)S(1)}, s32[2,1...) while((s32[]{:T(128)}, f32[2,6,80,1]{2,0,1,3:T(2,128)S(1)}, ...), condition=%wide.region_15.17_spmd.clone, body=%wide.region_13.16_spmd.clone.sunk | while | flops 160718496 | bytes 19275736 | solution.py:157
  188.3 3.7 fusion.208
  191.9 1.4 constant_dynamic-slice_fusion.34
  196.0 3.7 fusion.208
  199.6 1.4 constant_dynamic-slice_fusion.34
  203.7 2.3 broadcast_in_dim.274.clone
  206.0 34.5 %while.63 = (s32[]{:T(128)}, f32[2,80,6,64]{1,3,2,0:T(8,128)S(1)}, bf16[2,2,1280,384]{3,2,0,1:T(8,128)(2,1)}, bf16[2,2,1280,384]{2,3,1,0:T(8,128)(2,1)}, s32[2,1...) while((s32[]{:T(128)}, f32[2,80,6,64]{1,3,2,0:T(8,128)S(1)}, ...), condition=%wide.region_17.19_spmd.clone, body=%wide.region_16.18_spmd.clone.sunk | while | flops 401869536 | bytes 60658212 | solution.py:181
  206.0 4.3 fusion.221
  210.3 1.7 constant_dynamic-slice_fusion.37
  217.5 1.5 pad_maximum_fusion.5
  218.9 2.8 copy.95
  221.8 1.5 constant_dynamic-update-slice_fusion.2
  223.3 4.3 fusion.221
  227.6 1.7 constant_dynamic-slice_fusion.37
  234.7 1.5 pad_maximum_fusion.5
  236.2 2.8 copy.95
  239.1 1.5 constant_dynamic-update-slice_fusion.2
  241.7 2.2 bitcast_convert_fusion.1
  243.9 2.4 bitcast_convert_fusion
  248.2 128.4 %reduce-scatter.12.cloned.1.call-done = bf16[2,2,80,384]{3,2,0,1:T(8,128)(2,1)} async-done(((bf16[2,2,1280,384]{3,2,0,1:T(8,128)(2,1)}), bf16[2,2,80,384]{3,2,0,1:T(8,128)(2,1)}) %reduce-scatter.12.cloned.1.call-update) | async-done | bytes 245776 | tf_op jit(solution)/shard_map/reduce_scatter | solution.py:187
  376.6 2.4 fusion.85
  380.3 1.9 fusion.51
  387.3 2.5 all-reduce.6
  390.0 43.3 %all-reduce.4 = (f32[384]{0:T(512)}, f32[384]{0:T(512)}, f32[384]{0:T(512)}) all-reduce(f32[384]{0:T(512)S(1)} %dynamic-slice_convert_fusion.2, f32[384]{0:T(512)S(1)} %get-tuple-element.1100, f32[384]{0:T(512)S(1)} %get-tuple-element.1099), channel_id=1, replica_groups=mesh['seq'=16,'wa'=2] {'seq'}, use_global_device_ids=true, to_apply=%region_29.31 | all-reduce | flops 1152 | bytes 9216 | tf_op jit(solution)/shard_map/psum | solution.py:214
  434.4 2.1 scatter_custom_fusion.1
  437.4 186.6 %all-reduce.9.cloned.1.call-done = (bf16[3,768,384]{1,2,0:T(8,128)(2,1)}, bf16[384,768]{1,0:T(8,128)(2,1)}, bf16[768,1536]{1,0:T(8,128)(2,1)}, bf16[1536,768]{1,0:T(8,128)(2,1)}) async-done(((bf16[3,768,384]{1,2,0:T(8,128)(2,1)}, bf16[384,768]{1,0:T(8,128)(2,1)}, bf16[768,1536]{1,0:T(8,128)(2,1)}, bf16[1536,768]{1,0:T(8,128)(2,1)}), (bf16[3,768,384]{1,2,0:T(8,128)(2,1)}, bf16[384,768]{1,0:T(8,128)(2,1)}, ...) | async-done | bytes 7077904 | tf_op jit(solution)/shard_map/psum | solution.py:213
  624.0 4.1 copy.77
  629.2 4.6 convert_element_type.183
  633.8 2.5 convert_element_type.185
  (287 shorter events, 53.3 us)
Async XLA Ops:
  7.2 155.6 %copy-start = (bf16[1536,768]{1,0:T(8,128)(2,1)S(1)}, bf16[1536,768]{1,0:T(8,128)(2,1)}, u32[]{:S(2)}) copy-start(bf16[1536,768]{1,0:T(8,128)(2,1)} %param.26) | copy-start | bytes 7077892
  7.2 5.6 copy-start.59
  7.2 88.4 %all-gather.9.cloned.1.call-start = ((), (), s32[]{:S(2)}) async-start(), calls=%async_computation.5 | async-start | bytes 4177920 | tf_op jit(solution)/shard_map/all_gather | solution.py:74
  8.4 10.5 %copy-start.10 = (bf16[1,320,768]{2,1,0:T(8,128)(2,1)}, bf16[1,320,768]{2,1,0:T(8,128)(2,1)S(1)}, u32[]{:S(2)}) copy-start(bf16[1,320,768]{2,1,0:T(8,128)(2,1)S(1)} %copy.134) | copy-start | bytes 1474564
  9.2 5.5 copy-start.43
  9.2 10.8 %copy-start.35 = (s32[2,1280]{1,0:T(2,128)S(1)}, s32[2,1280]{1,0:T(2,128)}, u32[]{:S(2)}) copy-start(s32[2,1280]{1,0:T(2,128)} %param.30) | copy-start | bytes 30724
  10.0 16.5 %copy-start.4 = (bf16[80,768]{1,0:T(8,128)(2,1)}, bf16[80,768]{1,0:T(8,128)(2,1)S(1)}, u32[]{:S(2)}) copy-start(bf16[80,768]{1,0:T(8,128)(2,1)S(1)} %gather_fusion.3) | copy-start | bytes 368644
  10.0 10.6 %copy-start.42 = (s32[2,16]{1,0:T(2,128)S(1)}, s32[2,16]{1,0:T(2,128)}, u32[]{:S(2)}) copy-start(s32[2,16]{1,0:T(2,128)} %param.31) | copy-start | bytes 388
  12.8 14.5 %copy-start.20 = (bf16[160,768]{1,0:T(8,128)(2,1)}, bf16[160,768]{1,0:T(8,128)(2,1)S(1)}, u32[]{:S(2)}) copy-start(bf16[160,768]{1,0:T(8,128)(2,1)S(1)} %all-gather) | copy-start | bytes 737284
  14.7 12.8 %copy-start.40 = (f32[768]{0:T(1024)}, f32[768]{0:T(1024)S(1)}, u32[]{:S(2)}) copy-start(f32[768]{0:T(1024)S(1)} %reshape.509) | copy-start | bytes 9220
  18.9 136.3 %reduce-scatter.6.cloned.1.call-start = ((), (), s32[]{:S(2)}) async-start(), calls=%async_computation.6 | async-start | bytes 737280 | tf_op jit(solution)/shard_map/reduce_scatter | solution.py:115
  140.6 8.5 %copy-start.8 = (bf16[1,320,768]{2,1,0:T(8,128)(2,1)S(1)}, bf16[1,320,768]{2,1,0:T(8,128)(2,1)}, u32[]{:S(2)}) copy-start(bf16[1,320,768]{2,1,0:T(8,128)(2,1)} %param.22) | copy-start | bytes 1474564
  140.6 11.1 %copy-start.31 = (bf16[80,768]{1,0:T(8,128)(2,1)S(1)}, bf16[80,768]{1,0:T(8,128)(2,1)}, u32[]{:S(2)}) copy-start(bf16[80,768]{1,0:T(8,128)(2,1)} %copy-done.30) | copy-start | bytes 368644
  140.6 12.5 %copy-start.44 = (pred[80]{0:T(512)(128)(4,1)S(1)}, pred[80]{0:T(512)(128)(4,1)}, u32[]{:S(2)}) copy-start(pred[80]{0:T(512)(128)(4,1)} %copy-done.43) | copy-start | bytes 244
  140.6 14.7 %copy-start.5 = (bf16[80,768]{1,0:T(8,128)(2,1)S(1)}, bf16[80,768]{1,0:T(8,128)(2,1)}, u32[]{:S(2)}) copy-start(bf16[80,768]{1,0:T(8,128)(2,1)} %copy-done.4) | copy-start | bytes 368644
  144.5 26.0 %reduce-scatter.8.cloned.1.call-start = ((), (), s32[]{:S(2)}) async-start(), calls=%async_computation.7 | async-start | bytes 368640 | tf_op jit(solution)/shard_map/reduce_scatter | solution.py:123
  149.9 11.9 %copy-start.24 = (bf16[80,768]{1,0:T(8,128)(2,1)}, bf16[80,768]{1,0:T(8,128)(2,1)S(1)}, u32[]{:S(2)}) copy-start(bf16[80,768]{1,0:T(8,128)(2,1)S(1)} %gather_fusion.4) | copy-start | bytes 368644
  151.7 10.1 %copy-start.46 = (bf16[2,1,384]{2,1,0:T(2,128)(2,1)}, bf16[2,1,384]{2,1,0:T(2,128)(2,1)S(1)}, u32[]{:S(2)}) copy-start(bf16[2,1,384]{2,1,0:T(2,128)(2,1)S(1)} %all-gather.4) | copy-start | bytes 4612
  153.1 2.2 copy-start.53
  156.5 27.8 %copy-start.50 = (f32[80]{0:T(128)}, f32[80]{0:T(128)S(1)}, u32[]{:S(2)}) copy-start(f32[80]{0:T(128)S(1)} %add_rsqrt_fusion.1) | copy-start | bytes 964
  159.5 4.7 copy-start.15
  161.8 0.9 copy-start.33
  164.2 18.1 %reduce-scatter.10.cloned.1.call-start = ((), (), s32[]{:S(2)}) async-start(), calls=%async_computation.8 | async-start | bytes 737280 | tf_op jit(solution)/shard_map/reduce_scatter | solution.py:140
  164.3 2.7 copy-start.6
  166.9 1.8 copy-start.22
  167.0 15.4 %copy-start.7 = (f32[1,80,768]{2,1,0:T(8,128)S(1)}, f32[1,80,768]{2,1,0:T(8,128)}, u32[]{:S(2)}) copy-start(f32[1,80,768]{2,1,0:T(8,128)} %reduce-scatter.6.cloned.1.call-done) | copy-start | bytes 737284
  167.0 15.4 %copy-start.25 = (bf16[80,768]{1,0:T(8,128)(2,1)S(1)}, bf16[80,768]{1,0:T(8,128)(2,1)}, u32[]{:S(2)}) copy-start(bf16[80,768]{1,0:T(8,128)(2,1)} %copy-done.24) | copy-start | bytes 368644
  167.0 17.3 %copy-start.54 = (f32[80]{0:T(128)S(1)}, f32[80]{0:T(128)}, u32[]{:S(2)}) copy-start(f32[80]{0:T(128)} %copy-done.53) | copy-start | bytes 964
  167.0 20.6 %copy-start.14 = (bf16[384,768]{1,0:T(8,128)(2,1)S(1)}, bf16[384,768]{1,0:T(8,128)(2,1)}, u32[]{:S(2)}) copy-start(bf16[384,768]{1,0:T(8,128)(2,1)} %param.24) | copy-start | bytes 1769476
  168.7 19.4 %copy-start.38 = (f32[2,6,80,1]{2,1,0,3:T(8,128)S(1)}, f32[2,6,80,1]{2,1,0,3:T(8,128)}, u32[]{:S(2)}) copy-start(f32[2,6,80,1]{2,1,0,3:T(8,128)} %get-tuple-element.1591) | copy-start | bytes 11524
  168.7 207.9 %reduce-scatter.12.cloned.1.call-start = ((), (), s32[]{:S(2)}) async-start(), calls=%async_computation.9 | async-start | bytes 4177920 | tf_op jit(solution)/shard_map/reduce_scatter | solution.py:187
  184.3 4.0 copy-start.56
  212.5 2.0 copy-start.2
  214.5 1.7 copy-start.3
  229.8 2.0 copy-start.2
  231.8 1.7 copy-start.3
  240.5 0.9 copy-start.16
  240.5 1.2 copy-start.23
  240.6 3.4 copy-start.39
  240.6 192.7 %reduce-scatter.14.cloned.1.call-start = ((), (), s32[]{:S(2)}) async-start(), calls=%async_computation.10 | async-start | bytes 368640 | tf_op jit(solution)/shard_map/reduce_scatter | solution.py:195
  241.7 2.2 copy-start.34
  243.9 132.7 %copy-start.21 = (bf16[160,768]{1,0:T(8,128)(2,1)S(1)}, bf16[160,768]{1,0:T(8,128)(2,1)}, u32[]{:S(2)}) copy-start(bf16[160,768]{1,0:T(8,128)(2,1)} %copy-done.20) | copy-start | bytes 737284
  243.9 132.7 %copy-start.26 = (bf16[3,768,384]{2,1,0:T(8,128)(2,1)S(1)}, bf16[3,768,384]{2,1,0:T(8,128)(2,1)}, u32[]{:S(2)}) copy-start(bf16[3,768,384]{2,1,0:T(8,128)(2,1)} %param.23) | copy-start | bytes 5308420
  243.9 132.7 %copy-start.49 = (f32[2,80]{1,0:T(2,128)S(1)}, f32[2,80]{1,0:T(2,128)}, u32[]{:S(2)}) copy-start(f32[2,80]{1,0:T(2,128)} %copy-done.48) | copy-start | bytes 1924
  246.4 132.7 %copy-start.19 = (bf16[160,768]{1,0:T(8,128)(2,1)S(1)}, bf16[160,768]{1,0:T(8,128)(2,1)}, u32[]{:S(2)}) copy-start(bf16[160,768]{1,0:T(8,128)(2,1)} %copy-done.18) | copy-start | bytes 737284
  246.4 132.7 %copy-start.28 = (bf16[2,80,6,64]{1,3,2,0:T(8,128)(2,1)S(1)}, bf16[2,80,6,64]{1,3,2,0:T(8,128)(2,1)}, u32[]{:S(2)}) copy-start(bf16[2,80,6,64]{1,3,2,0:T(8,128)(2,1)} %copy-done.27) | copy-start | bytes 368644
  246.4 133.9 %copy-start.41 = (f32[768]{0:T(1024)S(1)}, f32[768]{0:T(1024)}, u32[]{:S(2)}) copy-start(f32[768]{0:T(1024)} %copy-done.40) | copy-start | bytes 9220
  376.6 3.7 copy-start.61
  379.0 245.0 %all-reduce.9.cloned.1.call-start = ((), (), s32[]{:S(2)}) async-start(), calls=%async_computation.11 | async-start | bytes 14155776 | tf_op jit(solution)/shard_map/psum | solution.py:213
  382.2 2.8 copy-start.9
  382.2 2.8 copy-start.11
  382.2 2.8 copy-start.37
  382.2 2.8 copy-start.45
  382.2 2.8 copy-start.55
  382.3 4.1 copy-start.58
  382.3 4.1 copy-start.60
  382.3 4.8 copy-start.32
  382.3 52.1 %copy-start.17 = (f32[1,80,768]{2,1,0:T(8,128)S(1)}, f32[1,80,768]{2,1,0:T(8,128)}, u32[]{:S(2)}) copy-start(f32[1,80,768]{2,1,0:T(8,128)} %reduce-scatter.10.cloned.1.call-done) | copy-start | bytes 737284
  382.3 52.1 %copy-start.51 = (f32[80]{0:T(128)S(1)}, f32[80]{0:T(128)}, u32[]{:S(2)}) copy-start(f32[80]{0:T(128)} %copy-done.50) | copy-start | bytes 964
  382.3 52.1 %copy-start.57 = (f32[80]{0:T(128)S(1)}, f32[80]{0:T(128)}, u32[]{:S(2)}) copy-start(f32[80]{0:T(128)} %copy-done.56) | copy-start | bytes 964
  386.4 241.7 %copy-start.12 = (bf16[320,768]{1,0:T(8,128)(2,1)}, bf16[320,768]{1,0:T(8,128)(2,1)S(1)}, u32[]{:S(2)}) copy-start(bf16[320,768]{1,0:T(8,128)(2,1)S(1)} %scatter_custom_fusion) | copy-start | bytes 1474564
  624.0 4.1 copy-start.36
  629.2 4.7 copy-start.13
  633.8 2.6 copy-start.1
  (8 other events, 5.5 us)
Sparse Core Ops, SparseCore 0:
  19.1 76.5 all-gather.8
  144.7 6.4 reduce-scatter.5
  164.4 6.1 reduce-scatter.7
  173.3 9.0 reduce-scatter.9
  240.7 135.8 reduce-scatter.11
  379.1 6.7 reduce-scatter.13
  393.0 230.9 all-reduce.8

commit v2 on v1

--- a/solution.py
+++ b/solution.py
@@ -1,14 +1,894 @@
+import functools
+
 import jax
 import jax.numpy as jnp
 from jax import lax
+from jax.experimental import pallas as pl
+from jax.experimental.pallas import tpu as pltpu
 from jax.sharding import PartitionSpec as P
 
 HD = 64
-CAP = 80
-
-
 EPS = 1e-05
 NEG = -1e30
+FAR = 1e9
+LINES = 4
+MESSAGES = 200
+VMEM_BYTES = 64 << 20
+MESH = pl.DeviceIdType.MESH
+F32 = jnp.float32
+BF16 = jnp.bfloat16
+NN = (((1,), (0,)), ((), ()))
+NT = (((1,), (1,)), ((), ()))
+TN = (((0,), (0,)), ((), ()))
+GELU_A = 0.7978845608028654
+GELU_B = 0.044715
+
+
+def mm(a, b, dims=NN):
+    return lax.dot_general(a, b, dims, preferred_element_type=F32)
+
+
+def gelu_parts(pre):
+    square = pre * pre
+    t = jnp.tanh(GELU_A * pre * (1.0 + GELU_B * square))
+    half = 0.5 * (1.0 + t)
+    slope = half + 0.5 * pre * (1.0 - t * t) * (GELU_A * (1.0 + 3.0 * GELU_B * square))
+    return pre * half, slope
+
+
+def row_scale(value):
+    return lax.rsqrt(jnp.mean(value * value, axis=-1, keepdims=True) + EPS)
+
+
+class Message:
+    def __init__(self, links, i, ends):
+        self.links, self.i, self.ends = links, i, ends
+
+    def make(self):
+        src, dst, device = self.ends()
+        return pltpu.make_async_remote_copy(
+            src_ref=src,
+            dst_ref=dst,
+            send_sem=self.links.send.at[self.i],
+            recv_sem=self.links.recv.at[self.i],
+            device_id=device,
+            device_id_type=MESH,
+        )
+
+    def start(self):
+        self.make().start()
+        self.links.pending.append(self)
+        return self
+
+    def wait_recv(self):
+        self.make().wait_recv()
+
+    def wait_send(self):
+        self.links.pending = [m for m in self.links.pending if m is not self]
+        self.make().wait_send()
+
+    def wait(self):
+        self.wait_send()
+        self.wait_recv()
+
+
+class Links:
+    def __init__(self, send, recv):
+        self.send, self.recv, self.used, self.pending = send, recv, 0, []
+
+    def message(self, ends):
+        self.used += 1
+        return Message(self, self.used - 1, ends)
+
+    def copy(self, ends):
+        return self.message(ends).start()
+
+    def drain(self):
+        for message in list(self.pending):
+            message.wait_send()
+
+
+class Place:
+    def __init__(self, nz):
+        self.me, self.c = lax.axis_index("seq"), lax.axis_index("wa")
+        self.nz = nz
+        self.z, self.l = lax.div(self.me, LINES), lax.rem(self.me, LINES)
+        y, x = lax.div(self.l, 2), lax.rem(self.l, 2)
+        over_y, over_x = self.l + 2 - 4 * y, self.l + 1 - 2 * x
+        self.l2 = over_y * (1 - self.c) + over_x * self.c
+        self.l3 = over_x * (1 - self.c) + over_y * self.c
+        self.l23 = 3 - self.l
+        self.sibling = (self.me, 1 - self.c)
+        self.ks = (1, 3, 2) if nz == 4 else tuple(range(1, nz))
+
+    def around(self, k):
+        return lax.rem(self.z + k, self.nz)
+
+    def at(self, z, line):
+        return (z * LINES + line, self.c)
+
+
+class Gather:
+    def __init__(self, place, links, buf, lend, own=False):
+        self.p, self.buf, self.lend, self.own = place, buf, lend, own
+        p, ks = place, (0, *place.ks)
+
+        def message(line, k, device):
+            def ends():
+                shard = buf().at[p.around(p.nz - k), line]
+                return shard, shard, device()
+
+            return links.message(ends)
+
+        lines = (p.l, p.l2, p.l3, p.l23)
+        self.first = {k: message(p.l, 0, lambda k=k: p.at(p.around(k), p.l)) for k in p.ks}
+        self.second = {k: message(p.l, k, lambda: p.at(p.z, p.l2)) for k in ks}
+        self.third = {(j, k): message(lines[j], k, lambda: p.at(p.z, p.l3)) for j in range(2) for k in ks}
+        self.lent = {}
+        if lend:
+            keys = [(j, k) for j in range(4) for k in ks if j or k or own]
+            self.lent = {key: message(lines[key[0]], key[1], lambda: p.sibling) for key in keys}
+        self.waited = set()
+
+    def hand_over(self, *key):
+        if key in self.lent:
+            self.lent[key].start()
+
+    def start(self):
+        self.hand_over(0, 0)
+        self.second[0].start()
+        self.third[0, 0].start()
+        for k in self.p.ks:
+            self.first[k].start()
+
+    def from_z(self, k):
+        self.first[k].wait_recv()
+        self.third[0, k].start()
+        self.second[k].start()
+        self.hand_over(0, k)
+
+    def from_second(self, k):
+        self.second[k].wait_recv()
+        self.third[1, k].start()
+        self.hand_over(1, k)
+
+    def from_third(self, j, k):
+        self.third[j, k].wait_recv()
+        self.hand_over(2 + j, k)
+
+    def lent_line(self, j):
+        for k in range(self.p.nz):
+            if (j, k) in self.lent and (j, k) not in self.waited:
+                self.waited.add((j, k))
+                self.lent[j, k].wait_recv()
+
+    def steps(self):
+        ks = self.p.ks
+        out = [functools.partial(self.from_z, k) for k in ks]
+        out += [functools.partial(self.from_second, k) for k in (0, *ks)]
+        out += [functools.partial(self.from_third, j, k) for j in range(2) for k in (0, *ks)]
+        return out
+
+
+class Scatter:
+    def __init__(self, place, links, acc, got1, got2, got3):
+        self.p = p = place
+        self.acc, self.got1, self.got2, self.got3 = acc, got1, got2, got3
+        self.order = (2, 1, 3, 0) if p.nz == 4 else (*range(1, p.nz), 0)
+
+        def one(o, j, line):
+            return lambda: (acc().at[p.around(o), line], got1().at[p.around(o), j], p.at(p.z, p.l3))
+
+        def two(o):
+            return lambda: (acc().at[p.around(o), p.l2], got2().at[p.around(o)], p.at(p.z, p.l2))
+
+        def three(o):
+            return lambda: (acc().at[p.around(o), p.l], got3().at[o - 1], p.at(p.around(o), p.l))
+
+        self.m1 = {
+            (j, o): links.message(one(o, j, line)) for o in self.order for j, line in ((0, p.l23), (1, p.l3))
+        }
+        self.m2 = {o: links.message(two(o)) for o in self.order}
+        self.m3 = {o: links.message(three(o)) for o in range(1, p.nz)}
+
+    def add(self, z, line, got):
+        acc = self.acc()
+        acc[z, line] = (acc[z, line].astype(F32) + got.astype(F32)).astype(BF16)
+
+    def start(self):
+        for message in self.m1.values():
+            message.start()
+
+    def stage2(self, o):
+        p, zz = self.p, self.p.around(o)
+        self.m1[0, o].wait_recv()
+        self.add(zz, p.l2, self.got1()[zz, 0])
+        self.m2[o].start()
+        self.m1[1, o].wait_recv()
+        self.add(zz, p.l, self.got1()[zz, 1])
+
+    def stage3(self, o):
+        p, zz = self.p, self.p.around(o)
+        self.m2[o].wait_recv()
+        if o:
+            self.add(zz, p.l, self.got2()[zz])
+            self.m3[o].start()
+
+    def total(self):
+        p = self.p
+        total = self.acc()[p.z, p.l].astype(F32) + self.got2()[p.z].astype(F32)
+        for o in range(1, p.nz):
+            self.m3[o].wait_recv()
+            total = total + self.got3()[o - 1].astype(F32)
+        return total
+
+    def steps(self):
+        out = [functools.partial(self.stage2, self.order[0])]
+        for now, before in zip(self.order[1:], self.order):
+            out += [functools.partial(self.stage2, now), functools.partial(self.stage3, before)]
+        return out + [functools.partial(self.stage3, self.order[-1])]
+
+
+def layer_kernel(
+    nz,
+    tokens, cot, picked, counts, gain_a_r, gain_m_r, router_r, wqkv_h, wout_h, wup_h, wdown_h,
+    pick_o, rows_o, grow_o, res_o, gup_o, gdown_o, small_o,
+    wqkv, wout, wup, wdown, wsem,
+    gvec, xall, uall, kall, vall, qst, bias, probs, att,
+    dyb, attn_s, resid_s, logit_s, part, got_a, got_m,
+    wall, gall, pre_s, act_s, gpre_s, dost, gq, gkv,
+    gsib, gu1, gu2, gu3, share, sh1, sh2, sh3, res,
+    sm, smz, smy, smx, smw, stage_u, stage_d, osem,
+    send, recv,
+):
+    place = Place(nz)
+    links = Links(send, recv)
+    c, l, z = place.c, place.l, place.z
+    other = 1 - c
+    rows, width = grow_o.shape
+    both = 2 * rows
+    block = tokens.shape[0]
+    half = wout.shape[0]
+    pairs = half // 128
+    nseq = nz * LINES
+    total_rows = nseq * rows
+    ff = wup.shape[1]
+    ks = place.ks
+
+    barrier = pltpu.get_barrier_semaphore()
+    peers = [place.at(place.around(k), l) for k in range(1, nz)]
+    peers += [place.at(z, place.l2), place.at(z, place.l3), place.sibling]
+    for peer in peers:
+        pl.semaphore_signal(barrier, inc=1, device_id=peer, device_id_type=MESH)
+    loads = [
+        pltpu.make_async_copy(h, v, wsem.at[i])
+        for i, (h, v) in enumerate(((wqkv_h, wqkv), (wout_h, wout), (wup_h, wup), (wdown_h, wdown)))
+    ]
+    for load in loads:
+        load.start()
+
+    itself = lax.broadcasted_iota(jnp.int32, (rows, total_rows), 1) == (
+        lax.broadcasted_iota(jnp.int32, (rows, total_rows), 0) + place.me * rows
+    )
+    picked_f = picked[...].astype(F32)
+    own_index = [
+        jnp.sum(jnp.where(itself, picked_f[s : s + 1], 0.0), axis=-1, keepdims=True) for s in range(2)
+    ]
+    own_row = jnp.where(c == 0, own_index[0], own_index[1])
+    pick = jnp.where(
+        lax.broadcasted_iota(jnp.int32, (rows, block), 1).astype(F32) == own_row, 1.0, 0.0
+    ).astype(BF16)
+    pick_o[...] = pick
+    xall[c, z, l] = mm(pick, tokens[...]).astype(BF16)
+    gvec[c] = jnp.zeros(gvec.shape[1:], F32)
+    for i, ref in enumerate((gain_a_r, gain_m_r, router_r)):
+        gvec[c, i : i + 1] = ref[...].astype(F32).reshape(1, half)
+    pl.semaphore_wait(barrier, len(peers))
+
+    gx = Gather(place, links, lambda: xall.at[c], True, own=True)
+    gx.start()
+    vec_copy = links.copy(lambda: (gvec.at[c], gvec.at[c], place.sibling))
+    dyb[c] = mm(pick, cot[...]).astype(BF16)
+    dy_copy = links.copy(lambda: (dyb.at[c], dyb.at[c], place.sibling))
+
+    lane = lax.broadcasted_iota(jnp.int32, (2, total_rows), 1)
+    stream = lax.broadcasted_iota(jnp.int32, (2, total_rows), 0)
+
+    def place_keys(d, carry):
+        until = d * rows + jnp.where(stream == 0, counts[0, d], counts[1, d])
+        mine = (lane >= d * rows) & (lane < until)
+        return jnp.where(mine, picked_f * nseq + d.astype(F32), carry)
+
+    kpos = lax.fori_loop(0, nseq, place_keys, jnp.full((2, total_rows), FAR, F32))
+    for s in range(2):
+        near = kpos[s : s + 1] <= own_index[s] * nseq + place.me.astype(F32)
+        bias[s] = jnp.where(near | itself, 0.0, NEG)
+    slot = lax.broadcasted_iota(jnp.int32, (both, 1), 0)
+    first = slot < rows
+    own_live = jnp.where(
+        slot - jnp.where(first, 0, rows) < jnp.where(first, counts[0, place.me], counts[1, place.me]), 1.0, 0.0
+    )
+    on_core = jnp.where(first, (1 - c).astype(F32), c.astype(F32))
+    vec_copy.wait_recv()
+    vectors = jnp.concatenate([gvec[0], gvec[1]], axis=1)
+    gain_a, gain_m, router = vectors[0:1], vectors[1:2], vectors[2:3]
+    loads[0].wait()
+
+    def project(s, line):
+        def norm(zz, carry):
+            value = xall[s, zz, line].astype(F32)
+            uall[s, zz, line] = (value * row_scale(value) * gain_a).astype(BF16)
+            return carry
+
+        lax.fori_loop(0, nz, norm, 0)
+        u = jnp.concatenate([uall[s, zz, line] for zz in range(nz)], axis=0)
+        for j, out in ((1, kall), (2, vall)):
+            value = mm(u, wqkv[j]).astype(BF16)
+            for p in range(pairs):
+                for zz in range(nz):
+                    out[s * pairs + p, zz, line] = value[
+                        zz * rows : (zz + 1) * rows, p * 128 : (p + 1) * 128
+                    ]
+
+    def arrive(j):
+        if j == 0:
+            for k in ks:
+                gx.from_z(k)
+        if j == 1:
+            for k in (0, *ks):
+                gx.from_second(k)
+            gx.lent_line(0)
+        if j == 3:
+            gx.lent_line(1)
+        if j == 4:
+            for k in (0, *ks):
+                gx.from_third(0, k)
+        if j == 5:
+            gx.lent_line(2)
+        if j == 6:
+            for k in (0, *ks):
+                gx.from_third(1, k)
+        if j == 7:
+            gx.lent_line(3)
+
+    def take_line(j, carry):
+        for i in (0, 1, 3, 4, 5, 6, 7):
+            pl.when(j == i)(functools.partial(arrive, i))
+        mine = lax.rem(j, 2) == 0
+        step = lax.div(j, 2)
+        one, two = jnp.where(mine, place.l2, place.l3), jnp.where(mine, place.l3, place.l2)
+        line = jnp.where(
+            step == 0, l, jnp.where(step == 1, one, jnp.where(step == 2, two, place.l23))
+        )
+        project(jnp.where(mine, c, other), line)
+        return carry
+
+    lax.fori_loop(0, 8, take_line, 0)
+    early = links.used
+    low = lax.broadcasted_iota(jnp.int32, (rows, 128), 1) < HD
+
+    def stacked(value, s, p):
+        piece = value[s * rows : (s + 1) * rows, p * 128 : (p + 1) * 128]
+        zero = jnp.zeros_like(piece)
+        return jnp.concatenate([jnp.where(low, piece, zero), jnp.where(low, zero, piece)], axis=0)
+
+    own_u = uall[:, z, l].reshape(both, width)
+    query = mm(own_u, wqkv[0]).astype(BF16) * jnp.asarray(HD ** (-0.5), BF16)
+    for s in range(2):
+        for p in range(pairs):
+            qst[s * pairs + p] = stacked(query, s, p)
+
+    def attend(i, carry):
+        s, p = lax.div(i, pairs), lax.rem(i, pairs)
+        keys = kall[i].reshape(total_rows, 128)
+        vals = vall[i].reshape(total_rows, 128)
+        hide = bias[s]
+        raw = mm(qst[i], keys, NT) + jnp.concatenate([hide, hide], axis=0)
+        expd = jnp.exp(raw - jnp.max(raw, axis=-1, keepdims=True))
+        prob = expd * (1.0 / jnp.sum(expd, axis=-1, keepdims=True))
+        probs[i] = prob
+        out = mm(prob.astype(BF16), vals)
+        at = pl.multiple_of(p * 128, 128)
+        att[s, :, pl.ds(at, 128)] = jnp.where(low, out[:rows], out[rows:]).astype(BF16)
+        return carry
+
+    lax.fori_loop(0, 2 * pairs, attend, 0)
+    loads[1].wait()
+    part[...] = mm(att[...].reshape(both, half), wout[...])
+    swap = links.copy(lambda: (part, got_a, place.sibling))
+    x_both = xall[:, z, l].reshape(both, width).astype(F32)
+    weight = jax.nn.sigmoid(jnp.sum(x_both * router, axis=-1, keepdims=True))
+    lift = weight * own_live
+    dy_copy.wait_recv()
+    swap.wait()
+    attn = part[...] + got_a[...]
+    attn_s[...] = attn
+    resid = x_both + attn
+    resid_s[...] = resid
+    w_both = (resid * row_scale(resid) * gain_m).astype(BF16)
+    wall[:, z, l] = w_both.reshape(2, rows, width)
+    gw = Gather(place, links, lambda: wall.at[c], True)
+    gw.start()
+    todo = gw.steps()
+
+    def pump(n):
+        for _ in range(min(n, len(todo))):
+            todo.pop(0)()
+
+    for load in loads[2:]:
+        load.wait()
+
+    fb = 384
+    for b in range(ff // fb):
+        cut = slice(b * fb, (b + 1) * fb)
+        pre = mm(w_both, wup[:, cut])
+        pre_s[:, cut] = pre
+        act_s[:, cut] = gelu_parts(pre)[0].astype(BF16)
+    pump(3)
+    part[...] = mm(act_s[...], wdown[...])
+    swap = links.copy(lambda: (part, got_m, place.sibling))
+    pump(2)
+    swap.wait()
+    branch = attn_s[...] + (part[...] + got_m[...])
+    x_both = xall[:, z, l].reshape(both, width).astype(F32)
+    dy_both = dyb[...].reshape(both, width).astype(F32)
+    grad_branch = dy_both * lift
+    g_both = grad_branch.astype(BF16)
+    gall[:, z, l] = g_both.reshape(2, rows, width)
+    gg = Gather(place, links, lambda: gall.at[c], True)
+    gg.start()
+    todo += gg.steps()
+    attn_s[...] = x_both + lift * branch
+    rows_o[...] = attn_s[pl.ds(pl.multiple_of(c * rows, rows), rows), :].astype(BF16)
+    grad_logit = (
+        jnp.sum(dy_both * branch, axis=-1, keepdims=True) * own_live * weight * (1.0 - weight)
+    )
+    logit_s[...] = grad_logit
+    sm[...] = jnp.zeros_like(sm)
+    sm[2:3] = jnp.sum(grad_logit * on_core * x_both, axis=0, keepdims=True)
+    pump(2)
+    for b in range(ff // fb):
+        cut = slice(b * fb, (b + 1) * fb)
+        grad_act = mm(g_both, wdown[cut, :], NT)
+        gpre_s[:, cut] = (gelu_parts(pre_s[:, cut])[1] * grad_act).astype(BF16)
+    pump(2)
+    part[...] = mm(gpre_s[...], wup[...], NT)
+    swap = links.copy(lambda: (part, got_a, place.sibling))
+    pump(2)
+    swap.wait()
+    grad_w = part[...] + got_a[...]
+    resid = resid_s[...]
+    scale_m = row_scale(resid)
+    hat = resid * scale_m
+    sm[1:2] = jnp.sum(grad_w * on_core * hat, axis=0, keepdims=True)
+    lifted = grad_w * gain_m
+    grad_resid = scale_m * (lifted - hat * jnp.mean(lifted * hat, axis=-1, keepdims=True))
+    resid_s[...] = grad_resid
+    ga_both = (dyb[...].reshape(both, width).astype(F32) * lift + grad_resid).astype(BF16)
+    attended = att[...].reshape(both, half)
+    piece = width // nseq
+    grad_o = mm(attended, ga_both, TN).astype(BF16)
+    for i in range(3):
+        value = jnp.concatenate(
+            [grad_o[:, 256 * i : 256 * i + 128], grad_o[:, 256 * i + 128 : 256 * i + 256]], axis=0
+        )
+        share[0, :, :, 0, i] = value.reshape(nz, LINES, piece, 128)
+    grad_att = mm(ga_both, wout[...], NT).astype(BF16)
+    for s in range(2):
+        for p in range(pairs):
+            dost[s * pairs + p] = stacked(grad_att, s, p)
+
+    scatters = [
+        Scatter(
+            place, links, lambda g=g: share.at[g], lambda g=g: sh1.at[g], lambda g=g: sh2.at[g], lambda g=g: sh3.at[g]
+        )
+        for g in range(2)
+    ]
+
+    def attend_back(s, p):
+        i = s * pairs + p
+        keys = kall[i].reshape(total_rows, 128)
+        vals = vall[i].reshape(total_rows, 128)
+        prob = probs[i]
+        grad_p = mm(dost[i], vals, NT)
+        delta = jnp.sum(grad_p * prob, axis=-1, keepdims=True)
+        grad_s = (prob * (grad_p - delta)).astype(BF16)
+        out = mm(grad_s, keys) * HD ** (-0.5)
+        gq[p, s] = jnp.where(low, out[:rows], out[rows:]).astype(BF16)
+        gkv[p, s, :, :128] = mm(grad_s, qst[i], TN).astype(BF16)
+        gkv[p, s, :, 128:] = mm(prob.astype(BF16), dost[i], TN).astype(BF16)
+
+    def share_pair(p):
+        group, unit = lax.div(p + 1, 2), lax.rem(p + 1, 2)
+        grad_q = mm(uall[:, z, l].reshape(both, width), gq[p].reshape(both, 128), TN)
+        share[group, :, :, unit, 0] = grad_q.astype(BF16).reshape(nz, LINES, piece, 128)
+        span = width // 2
+
+        def half_of(h, carry):
+            at = pl.ds(pl.multiple_of(h * span, span), span)
+            value = mm(uall[0, :, :, :, at].reshape(total_rows, span), gkv[p, 0], TN)
+            value = value + mm(uall[1, :, :, :, at].reshape(total_rows, span), gkv[p, 1], TN)
+            value = value.astype(BF16)
+            zs = pl.ds(h * (nz // 2), nz // 2)
+            for j in range(2):
+                share[group, zs, :, unit, 1 + j] = value[:, 128 * j : 128 * (j + 1)].reshape(
+                    nz // 2, LINES, piece, 128
+                )
+            return carry
+
+        lax.fori_loop(0, 2, half_of, 0)
+
+    counts_at = [3, 3, 3, 3, 3, 3]
+    queue = [[todo.pop(0) for _ in range(min(n, len(todo)))] for n in counts_at]
+    queue[-1] += todo
+    del todo[:]
+
+    def back(i, carry):
+        p, s = lax.div(i, 2), lax.rem(i, 2)
+        attend_back(s, p)
+        pl.when(s == 1)(lambda: share_pair(p))
+        for j, steps in enumerate(queue):
+
+            def go(steps=steps, j=j):
+                for step in steps:
+                    step()
+                if j == 1:
+                    scatters[0].start()
+                if j == 5:
+                    scatters[1].start()
+
+            pl.when(i == j)(go)
+        return carry
+
+    lax.fori_loop(0, 2 * pairs, back, 0)
+    for message in list(links.pending):
+        if message.i < early:
+            message.wait_send()
+
+    own_gq = jnp.concatenate([gq[p].reshape(both, 128) for p in range(pairs)], axis=1)
+    part[...] = mm(own_gq, wqkv[0], NT)
+
+    def grad_u(s, zz):
+        at = pl.ds(pl.multiple_of(zz * (LINES * rows), LINES * rows), LINES * rows)
+        gk = jnp.concatenate([gkv[p, s, at, :128] for p in range(pairs)], axis=1)
+        gv = jnp.concatenate([gkv[p, s, at, 128:] for p in range(pairs)], axis=1)
+        return mm(gk, wqkv[1], NT) + mm(gv, wqkv[2], NT)
+
+    def part_of(s):
+        return part[pl.ds(pl.multiple_of(s * rows, rows), rows), :]
+
+    def theirs(j, carry):
+        zz = place.around(j + 1)
+        xall[other, zz] = grad_u(other, zz).astype(BF16).reshape(LINES, rows, width)
+        return carry
+
+    lax.fori_loop(0, nz, theirs, 0)
+    xall[other, z, l] = (xall[other, z, l].astype(F32) + part_of(other)).astype(BF16)
+    lent = [
+        links.copy(
+            lambda j=j: (xall.at[other, place.around(j + 1)], gsib.at[place.around(j + 1)], place.sibling)
+        )
+        for j in range(nz)
+    ]
+
+    def ours(j, gain_total):
+        zz = place.around(j + 1)
+        value = grad_u(c, zz).reshape(LINES, rows, width)
+        for i in range(nz):
+            pl.when(j == i)(lent[i].wait_recv)
+        value = value + gsib[zz].astype(F32)
+        rows_x = xall[c, zz].astype(F32)
+        hat = rows_x * row_scale(rows_x)
+        xall[c, zz] = value.astype(BF16)
+        return gain_total + jnp.sum(value * hat, axis=(0, 1)).reshape(1, width)
+
+    x_own = xall[c, z, l].astype(F32)
+    gain_total = jnp.sum(part_of(c) * (x_own * row_scale(x_own)), axis=0, keepdims=True)
+    attn_s[pl.ds(0, rows), :] = x_own
+    gain_total = lax.fori_loop(0, nz, ours, gain_total)
+    xall[c, z, l] = (xall[c, z, l].astype(F32) + part_of(c)).astype(BF16)
+    sm[0:1] = gain_total
+    reduce_u = Scatter(place, links, lambda: xall.at[c], lambda: gu1, lambda: gu2, lambda: gu3)
+    reduce_u.start()
+    for j in range(LINES):
+        gw.lent_line(j)
+        gg.lent_line(j)
+
+    small = {
+        "y": links.message(lambda: (smy.at[0], smy.at[1], place.at(z, place.l2))),
+        "x": links.message(lambda: (smx.at[0], smx.at[1], place.at(z, place.l3))),
+        "w": links.message(lambda: (smw.at[0], smw.at[1], place.sibling)),
+    }
+    for k in range(1, nz):
+        small[k] = links.copy(
+            lambda k=k: (sm, smz.at[k - 1], place.at(place.around(k), l))
+        )
+
+    def small_z():
+        for k in range(1, nz):
+            small[k].wait_recv()
+        total = jnp.zeros(sm.shape, F32)
+        for source in range(nz):
+            for k in range(nz):
+                piece = sm[...] if k == 0 else smz[k - 1]
+                total = total + jnp.where(place.around(nz - k) == source, piece, 0.0)
+        smy[0] = total
+        small["y"].start()
+
+    def small_2():
+        small["y"].wait_recv()
+        smx[0] = smy[0] + smy[1]
+        small["x"].start()
+
+    def small_3():
+        small["x"].wait_recv()
+        smw[0] = smx[0] + smx[1]
+        small["w"].start()
+
+    def small_4():
+        small["w"].wait_recv()
+        total = smw[0] + smw[1]
+        small_o[...] = jnp.where(c == 0, total[:, :half], total[:, half:])
+
+    gathers = [Gather(place, links, lambda g=g: res.at[g], False) for g in range(2)]
+
+    def weights_out(g):
+        res[g, z, l] = scatters[g].total().astype(BF16)
+        gathers[g].start()
+
+    def tokens_out():
+        grad = reduce_u.total()
+        own = attn_s[pl.ds(0, rows), :]
+        scale = row_scale(own)
+        hat = own * scale
+        lifted = grad * gain_a
+        grad_x = scale * (lifted - hat * jnp.mean(lifted * hat, axis=-1, keepdims=True))
+        at = pl.ds(pl.multiple_of(c * rows, rows), rows)
+        grow_o[...] = grad_x + resid_s[at, :] + logit_s[at, :] * router
+
+    timed = []
+
+    def plan(steps, begin, end):
+        gap = (end - begin) / max(len(steps) - 1, 1)
+        timed.extend((begin + gap * i, step) for i, step in enumerate(steps))
+
+    plan(scatters[0].steps(), -3, -1)
+    plan([functools.partial(weights_out, 0)], -1, -1)
+    plan([small_z], 1, 1)
+    plan(scatters[1].steps(), 0, 4)
+    plan([functools.partial(weights_out, 1)], 4, 4)
+    plan(gathers[0].steps(), 1, 7)
+    plan(reduce_u.steps(), 3, 11)
+    plan(gathers[1].steps(), 6, 14)
+    plan([small_2, small_3, small_4], 5, 11)
+    plan([tokens_out], 12, 12)
+
+    slots, part_ff = stage_u.shape[:2]
+    hb = slots * part_ff
+    blocks = ff // hb
+    tile = total_rows // 2
+    tiles = 2 * total_rows // tile
+    points = (tiles + 2) * blocks
+    spread = [[] for _ in range(points + 1)]
+    for at, step in sorted(timed, key=lambda pair: pair[0]):
+        if at < 0:
+            step()
+        else:
+            spread[min(int(at), points)].append(step)
+
+    def put(b, i, which, stage, out):
+        at = pl.ds(pl.multiple_of(b * hb + i * part_ff, part_ff), part_ff)
+        return pltpu.make_async_copy(stage.at[i], out.at[at, :], osem.at[which, i])
+
+    def pumps(point, among):
+        for j in among:
+            if spread[j]:
+
+                def go(steps=spread[j]):
+                    for step in steps:
+                        step()
+
+                pl.when(point == j)(go)
+
+    def ff_block(b, carry):
+        cut = pl.ds(pl.multiple_of(b * hb, hb), hb)
+
+        def ff_tile(t, carry):
+            s, h = lax.div(t, 2), lax.rem(t, 2)
+            at = pl.ds(pl.multiple_of(h * tile, tile), tile)
+            zz = pl.ds(h * (nz // 2), nz // 2)
+            act, slope = gelu_parts(mm(wall[s, zz].reshape(tile, width), wup[:, cut]))
+            uall[s, zz, :, :, :hb] = act.astype(BF16).reshape(nz // 2, LINES, rows, hb)
+            grad_act = mm(gall[s, zz].reshape(tile, width), wdown[cut, :], NT)
+            grad_pre = (slope * grad_act).astype(BF16)
+            for i in range(slots):
+                gkv[i, s, at] = grad_pre[:, part_ff * i : part_ff * (i + 1)]
+            pumps(b * (tiles + 2) + t, [i for i in range(points) if i % (tiles + 2) < tiles])
+            return carry
+
+        lax.fori_loop(0, tiles, ff_tile, 0)
+
+        def flush(which, stage, out, lhs, rhs):
+            for i in range(slots):
+                pl.when(b >= 1)(lambda i=i: put(b - 1, i, which, stage, out).wait())
+                stage[i] = mm(lhs(i), rhs[...].reshape(2 * total_rows, width), TN).astype(BF16)
+                put(b, i, which, stage, out).start()
+
+        flush(
+            0, stage_d, gdown_o,
+            lambda i: uall[:, :, :, :, part_ff * i : part_ff * (i + 1)].reshape(2 * total_rows, part_ff), gall,
+        )
+        pumps(b * (tiles + 2) + tiles, range(tiles, points, tiles + 2))
+        flush(1, stage_u, gup_o, lambda i: gkv[i].reshape(2 * total_rows, part_ff), wall)
+        pumps(b * (tiles + 2) + tiles + 1, range(tiles + 1, points, tiles + 2))
+        return carry
+
+    lax.fori_loop(0, blocks, ff_block, 0)
+    for step in spread[points]:
+        step()
+    out_copy = pltpu.make_async_copy(res, res_o, osem.at[2, 0])
+    out_copy.start()
+    for i in range(slots):
+        put(blocks - 1, i, 0, stage_d, gdown_o).wait()
+        put(blocks - 1, i, 1, stage_u, gup_o).wait()
+    links.drain()
+    out_copy.wait()
+
+
+def finish_kernel(
+    tokens, cot, pick, rows, grow, small, res_h, gup_h, gdown_h,
+    mixed_o, gtok_o, gain_a_o, gain_m_o, router_o, gqkv_o, gout_o, gup_o, gdown_o,
+    res, gup, gdown, qkv_s, out_s, up_s, down_s, sem_in, sem_out,
+):
+    up_cuts = [slice(i * 384, (i + 1) * 384) for i in range(gup.shape[0] // 384)]
+    down_cuts = [slice(i * 384, (i + 1) * 384) for i in range(gdown.shape[0] // 384)]
+    loads, stores = [], []
+
+    def load(src, dst):
+        loads.append(pltpu.make_async_copy(src, dst, sem_in.at[len(loads)]))
+        loads[-1].start()
+        return loads[-1]
+
+    def store(src, dst):
+        stores.append(pltpu.make_async_copy(src, dst, sem_out.at[len(stores)]))
+        stores[-1].start()
+
+    downs = [load(gdown_h.at[cut], gdown.at[cut]) for cut in down_cuts]
+    groups = [load(res_h.at[g], res.at[g]) for g in range(2)]
+    ups = [load(gup_h.at[cut], gup.at[cut]) for cut in up_cuts]
+    for cut, got in zip(down_cuts, downs):
+        got.wait()
+        down_s[cut] = gdown[cut].astype(F32)
+        store(down_s.at[cut], gdown_o.at[cut])
+    width = rows.shape[1]
+    half = width // 2
+    for got in groups:
+        got.wait()
+    for i in range(3):
+        for unit in range(1, 4):
+            cut = slice((unit - 1) * 128, unit * 128)
+            qkv_s[i, :, cut] = res[unit // 2, :, :, unit % 2, i].reshape(width, 128).astype(F32)
+        store(qkv_s.at[i], gqkv_o.at[i])
+        value = res[0, :, :, 0, i].reshape(width, 128).astype(F32)
+        out_s[:, 256 * i : 256 * i + 128] = value[:half]
+        out_s[:, 256 * i + 128 : 256 * i + 256] = value[half:]
+    store(out_s, gout_o)
+    for cut, got in zip(up_cuts, ups):
+        got.wait()
+        up_s[:, cut] = gup[cut].astype(F32).T
+        store(up_s.at[:, cut], gup_o.at[:, cut])
+    chosen = mm(pick[...], jnp.ones(rows.shape, BF16), TN) > 0.5
+    mixed_o[...] = jnp.where(chosen, mm(pick[...], rows[...], TN), tokens[...].astype(F32)).astype(BF16)
+    grad = grow[...]
+    hi = grad.astype(BF16)
+    rest = grad - hi.astype(F32)
+    mid = rest.astype(BF16)
+    lo = (rest - mid.astype(F32)).astype(BF16)
+    spread = mm(pick[...], hi, TN) + (mm(pick[...], mid, TN) + mm(pick[...], lo, TN))
+    gtok_o[...] = (cot[...].astype(F32) + spread).astype(BF16)
+    gain_a_o[...] = small[0:1].reshape(half)
+    gain_m_o[...] = small[1:2].reshape(half)
+    router_o[...] = small[2:3].reshape(half)
+    for made in stores:
+        made.wait()
+
+
+def fused_body(
+    tokens, cotangent, w_qkv, w_out, w_up, w_down, gain_attn, gain_mlp, router, picked, counts
+):
+    nseq = lax.axis_size("seq")
+    nz = nseq // LINES
+    rows = picked.shape[1] // nseq
+    block, width = tokens.shape[1:]
+    half, ff = w_out.shape[0], w_up.shape[1]
+    pairs = half // 128
+    total_rows = nseq * rows
+    piece = width // nseq
+    vm = pltpu.VMEM
+    dma = pltpu.SemaphoreType.DMA
+    wide = (2, nz, LINES, rows, width)
+    heads = (2 * pairs, nz, LINES, rows, 128)
+    both = (2 * rows, width)
+    part = (2, 3, piece, 128)
+    scratch = [
+        vm((3, width, half), BF16), vm((half, width), BF16), vm((width, ff), BF16), vm((ff, width), BF16), dma((4,)),
+        vm((2, 8, half), F32), vm(wide, BF16), vm(wide, BF16), vm(heads, BF16), vm(heads, BF16),
+        vm((2 * pairs, 2 * rows, 128), BF16), vm((2, rows, total_rows), F32),
+        vm((2 * pairs, 2 * rows, total_rows), F32), vm((2, rows, half), BF16),
+        vm((2, rows, width), BF16), vm(both, F32), vm(both, F32), vm((2 * rows, 1), F32),
+        vm(both, F32), vm(both, F32), vm(both, F32),
+        vm(wide, BF16), vm(wide, BF16), vm((2 * rows, ff), F32), vm((2 * rows, ff), BF16), vm((2 * rows, ff), BF16),
+        vm((2 * pairs, 2 * rows, 128), BF16), vm((pairs, 2, rows, 128), BF16), vm((pairs, 2, total_rows, 256), BF16),
+        vm((nz, LINES, rows, width), BF16), vm((nz, 2, rows, width), BF16), vm((nz, rows, width), BF16),
+        vm((nz - 1, rows, width), BF16),
+        vm((2, nz, LINES, *part), BF16), vm((2, nz, 2, *part), BF16), vm((2, nz, *part), BF16),
+        vm((2, nz - 1, *part), BF16), vm((2, nz, LINES, *part), BF16),
+        vm((8, width), F32), vm((nz - 1, 8, width), F32), vm((2, 8, width), F32), vm((2, 8, width), F32),
+        vm((2, 8, width), F32),
+        vm((2, 256, width), BF16), vm((2, 256, width), BF16), dma((3, 2)),
+        dma((MESSAGES,)), dma((MESSAGES,)),
+    ]
+    in_vmem = pl.BlockSpec(memory_space=pltpu.VMEM)
+    in_hbm = pl.BlockSpec(memory_space=pl.ANY)
+    in_smem = pl.BlockSpec(memory_space=pltpu.SMEM)
+    shaped = jax.ShapeDtypeStruct
+    pick, out_rows, grad_rows, res, grad_up, grad_down, small = pl.pallas_call(
+        functools.partial(layer_kernel, nz),
+        out_shape=(
+            shaped((rows, block), BF16),
+            shaped((rows, width), BF16),
+            shaped((rows, width), F32),
+            shaped((2, nz, LINES, *part), BF16),
+            shaped((ff, width), BF16),
+            shaped((ff, width), BF16),
+            shaped((8, half), F32),
+        ),
+        in_specs=[in_vmem] * 3 + [in_smem] + [in_vmem] * 3 + [in_hbm] * 4,
+        out_specs=(in_vmem, in_vmem, in_vmem, in_hbm, in_hbm, in_hbm, in_vmem),
+        scratch_shapes=scratch,
+        compiler_params=pltpu.CompilerParams(
+            collective_id=0, has_side_effects=True, vmem_limit_bytes=VMEM_BYTES
+        ),
+        name="layer",
+    )(
+        tokens[0], cotangent[0], picked, counts,
+        gain_attn, gain_mlp, router, w_qkv, w_out, w_up, w_down,
+    )
+    mixed, grad_tokens, gain_a, gain_m, grad_r, grad_qkv, grad_out, grad_up, grad_down = pl.pallas_call(
+        finish_kernel,
+        out_shape=(
+            shaped((block, width), BF16),
+            shaped((block, width), BF16),
+            shaped((half,), F32),
+            shaped((half,), F32),
+            shaped((half,), F32),
+            shaped((3, width, half), F32),
+            shaped((half, width), F32),
+            shaped((width, ff), F32),
+            shaped((ff, width), F32),
+        ),
+        in_specs=[in_vmem] * 6 + [in_hbm] * 3,
+        out_specs=(in_vmem,) * 5 + (in_hbm,) * 4,
+        scratch_shapes=[
+            vm((2, nz, LINES, *part), BF16), vm((ff, width), BF16), vm((ff, width), BF16),
+            vm((3, width, half), F32), vm((half, width), F32), vm((width, ff), F32), vm((ff, width), F32),
+            dma((16,)), dma((16,)),
+        ],
+        compiler_params=pltpu.CompilerParams(vmem_limit_bytes=VMEM_BYTES),
+        name="finish",
+    )(tokens[0], cotangent[0], pick, out_rows, grad_rows, small, res, grad_up, grad_down)
+    return (
+        mixed[None], grad_tokens[None], grad_qkv, grad_out, grad_up, grad_down, gain_a, gain_m, grad_r,
+    )
+
+
+def body(tokens, *rest):
+    nseq, cores = lax.axis_size("seq"), lax.axis_size("wa")
+    fits = nseq == 4 * LINES and cores == 2 and rest[-2].shape[1] == nseq * CAP
+    return (fused_body if fits else spread_body)(tokens, *rest)
+
+
+CAP = 80
 
 
 def norm_rows(value, gain):
@@ -28,7 +908,7 @@
     return pull(grad)[0]
 
 
-def body(
+def spread_body(
     tokens, cotangent, w_qkv, w_out, w_up, w_down, gain_attn, gain_mlp, router, picked, counts
 ):
     f32 = jnp.float32

time: 645 us -> 180 us (0.28)
  waiting for transfers between devices: 397 us -> 0 us
  Pallas kernels: 0 us -> 179 us
  local copies, waits for them, and re-layouts: 88.5 us -> 0 us
  blocking collectives: 59.5 us -> 0 us
  matrix products: 44.7 us -> 0 us
  other arithmetic: 37.5 us -> 0 us
  between operations: 15.6 us -> 0.81 us
    psum x1 -> x0, waiting for transfers between devices: 187 us -> none  [body(): large = lax.psum(tuple((share.astype(bf16) for share in shares[:4])), 'seq')]
    pallas_call x0 -> x2, Pallas kernels: none -> 179 us  [the longest x1 169 us: fused_body(): pl.pallas_call(functools.partial(layer_kernel, nz), out_shape=(shaped((ro...]
    reduce_scatter x5 -> x0, waiting for transfers between devices: 142 us -> none  [the longest x1 128 us: body(): lax.psum_scatter(holder.astype(bf16), 'seq', scatter_dimension=2, tiled=T...]
    all_gather x1 -> x0, waiting for transfers between devices: 68 us -> none  [body(): kv_all = lax.all_gather(local_kv, 'seq', axis=2, tiled=True)]
    dot_general x32 -> x0, matrix products: 44.7 us -> none  [the longest x6 7.36 us: block_of(): jnp.einsum('sqhd,skhd->shqk', split_q, keys_b, preferred_element_type=f32)]
    psum x1 -> x0, blocking collectives: 43.3 us -> none  [body(): small = lax.psum(shares[4:], 'seq')]
    slice x11 -> x0, local copies, waits for them, and re-layouts: 29.7 us -> none  [the longest x6 19.3 us: block_of(): kv_all[0]]
    unnamed x132 -> x0, local copies, waits for them, and re-layouts: 19.9 us -> none
  transfers between devices with their start and end apart: 7 -> 0, of which waited for: 5 -> 0; matrix products, arithmetic and copies ran while one was open for 5% -> 0% of each run, Pallas kernels for 0% -> 0%
where the time goes in v2:
time: 180 us
  Pallas kernels  179 us (99%)
    pallas_call x1, Pallas kernels, fused_body(): pl.pallas_call(functools.partial(layer_kernel, nz), out_shape=(shaped((ro...  169 us
    pallas_call x1, Pallas kernels, fused_body(): pl.pallas_call(finish_kernel, out_shape=(shaped((block, width), BF16), sh...  9.63 us

profile of v2, /device:TPU:0, one launch (start us, length us, event | category | flops | bytes accessed | tf_op | source)
XLA Modules:
  0.0 179.6 jit_solution(10663274275113749509)
XLA Ops:
  0.6 169.2 %layer.1 = (bf16[80,320]{1,0:T(8,128)(2,1)}, bf16[80,768]{1,0:T(8,128)(2,1)}, f32[80,768]{1,0:T(8,128)}, bf16[2,4,4,2,3,48,128]{6,5,4,3,2,1,0:T(8,128)(2,1)}, bf...) custom-call(bf16[320,768]{1,0:T(8,128)(2,1)} %bitcast.4, bf16[320,768]{1,0:T(8,128)(2,1)} %bitcast.6, ...), custom_call_target="tpu_custom_call" | custom-call | tf_op jit(solution)/shard_map/layer/pallas_call | solution.py:835
  169.9 9.6 %finish.1 = (bf16[320,768]{1,0:T(8,128)(2,1)}, bf16[320,768]{1,0:T(8,128)(2,1)}, f32[384]{0:T(512)}, f32[384]{0:T(512)}, f32[384]{0:T(512)}, /*index=5*/f32[3,76...) custom-call(bf16[320,768]{1,0:T(8,128)(2,1)} %bitcast.5, bf16[320,768]{1,0:T(8,128)(2,1)} %bitcast.7, ...), custom_call_target="tpu_custom_call" | custom-call | tf_op jit(solution)/shard_map/finish/pallas_call | solution.py:857

commit v3 on v2

--- a/solution.py
+++ b/solution.py
@@ -12,8 +12,68 @@
 NEG = -1e30
 FAR = 1e9
 LINES = 4
-MESSAGES = 200
+MESSAGES = 420
 VMEM_BYTES = 64 << 20
+EARLY_ROWS = 48
+COTANGENT_AT = 1
+POINTS = {"x": 0, "a": 8, "p": 14, "b": 20, "v": 27, "u": 31, "h": 36, "z": 54}
+SCHEDULE = (
+    (0, 16, 21, 7, 15, 1, 2, 24, 22, 17, 18),
+    (23, 26, 5, 3),
+    (8, 6, 19, 4, 10, 27, 20),
+    (9, 25),
+    (30,),
+    (33, 45, 51, 37, 11, 31),
+    (28, 13, 52, 14, 29, 12),
+    (46,),
+    (56, 34, 38, 32, 48),
+    (41, 49, 53),
+    (35, 39),
+    (),
+    (47,),
+    (36, 40, 42),
+    (50, 57),
+    (54, 55),
+    (43,),
+    (44,),
+    (59,),
+    (60, 63),
+    (82, 75, 58, 67, 61, 81),
+    (64, 83, 71, 68),
+    (62,),
+    (86, 78, 65),
+    (155, 69, 76, 77, 79),
+    (150, 154, 157, 156, 80),
+    (72, 152),
+    (151, 153, 70),
+    (73, 87, 85),
+    (),
+    (66, 84),
+    (),
+    (168, 88, 163, 162),
+    (166,),
+    (),
+    (167, 169, 158, 164, 159, 89, 165, 74),
+    (160,),
+    (171, 161),
+    (188, 174),
+    (170, 176),
+    (186, 172),
+    (179, 178),
+    (181, 90, 175, 105, 91, 177, 180),
+    (111, 189, 173, 187),
+    (97, 106, 93, 112, 94),
+    (107, 182, 98, 113, 92),
+    (136, 135, 120, 108, 183, 121, 123, 95, 190, 109),
+    (99, 184, 115, 116, 127),
+    (114, 96),
+    (142, 102, 117, 100, 128, 125),
+    (141, 131, 118, 144, 185),
+    (122, 137, 133, 129, 101),
+    (110, 191, 126, 124, 103),
+    (143, 146, 145, 132, 130, 134, 139, 138),
+    (140, 192, 148, 147, 149, 119, 104),
+)
 MESH = pl.DeviceIdType.MESH
 F32 = jnp.float32
 BF16 = jnp.bfloat16
@@ -64,7 +124,7 @@
         self.make().wait_recv()
 
     def wait_send(self):
-        self.links.pending = [m for m in self.links.pending if m is not self]
+        self.links.forget(self)
         self.make().wait_send()
 
     def wait(self):
@@ -76,9 +136,18 @@
     def __init__(self, send, recv):
         self.send, self.recv, self.used, self.pending = send, recv, 0, []
 
+    def many(self, count):
+        self.used += count
+        return self.used - count
+
+    def numbered(self, i, ends):
+        return Message(self, i, ends)
+
+    def forget(self, what):
+        self.pending = [other for other in self.pending if other is not what]
+
     def message(self, ends):
-        self.used += 1
-        return Message(self, self.used - 1, ends)
+        return self.numbered(self.many(1), ends)
 
     def copy(self, ends):
         return self.message(ends).start()
@@ -99,7 +168,16 @@
         self.l3 = over_x * (1 - self.c) + over_y * self.c
         self.l23 = 3 - self.l
         self.sibling = (self.me, 1 - self.c)
-        self.ks = (1, 3, 2) if nz == 4 else tuple(range(1, nz))
+        near = [sorted(range(nz), key=lambda other: abs(other - here)) for here in range(nz)]
+        self.sources = []
+        for i in range(nz):
+            source = near[0][i] + 0 * self.z
+            for here in range(1, nz):
+                source = jnp.where(self.z == here, near[here][i], source)
+            self.sources.append(source)
+
+    def turn(self, i):
+        return self.sources[i]
 
     def around(self, k):
         return lax.rem(self.z + k, self.nz)
@@ -108,66 +186,121 @@
         return (z * LINES + line, self.c)
 
 
+class Chain:
+    def __init__(self, place, links, shard):
+        self.p, self.links, self.shard = place, links, shard
+        self.i = links.many(2 * place.nz)
+
+    def hop(self, source, to, down, hops):
+        i = self.i + down * self.p.nz + hops
+        return self.links.numbered(
+            i, lambda: (self.shard(source), self.shard(source), self.p.at(to, self.p.l))
+        )
+
+    def start(self):
+        p = self.p
+        pl.when(p.z + 1 < p.nz)(lambda: self.hop(p.z, p.z + 1, 0, 1).make().start())
+        pl.when(p.z > 0)(lambda: self.hop(p.z, p.z - 1, 1, 1).make().start())
+        self.links.pending.append(self)
+
+    def arrive(self, i):
+        p = self.p
+        source = p.turn(i)
+        down = jnp.where(source > p.z, 1, 0)
+        hops = jnp.where(source > p.z, source - p.z, p.z - source)
+        self.hop(source, p.z, down, hops).wait_recv()
+        on = p.z + 1 - 2 * down
+        pl.when((on >= 0) & (on < p.nz))(lambda: self.hop(source, on, down, hops + 1).make().start())
+
+    def wait_send(self):
+        p = self.p
+        self.links.forget(self)
+        for hops in range(1, p.nz):
+            up = (p.z + 1 < p.nz) & (p.z >= hops - 1)
+            down = (p.z > 0) & (p.z + hops - 1 < p.nz)
+            pl.when(up)(lambda: self.hop(p.z, p.z, 0, hops).make().wait_send())
+            pl.when(down)(lambda: self.hop(p.z, p.z, 1, hops).make().wait_send())
+
+
 class Gather:
-    def __init__(self, place, links, buf, lend, own=False):
-        self.p, self.buf, self.lend, self.own = place, buf, lend, own
-        p, ks = place, (0, *place.ks)
-
-        def message(line, k, device):
+    def __init__(self, place, links, buf, lend, own=False, early=True, cut=None):
+        self.p = p = place
+        self.early = early
+        lines = (p.l, p.l2, p.l3, p.l23)
+
+        def at(source, line):
+            ref = buf().at[source, line]
+            return ref if cut is None else ref.at[cut]
+
+        def message(j, i, device):
             def ends():
-                shard = buf().at[p.around(p.nz - k), line]
+                shard = at(p.turn(i), lines[j])
                 return shard, shard, device()
 
             return links.message(ends)
 
-        lines = (p.l, p.l2, p.l3, p.l23)
-        self.first = {k: message(p.l, 0, lambda k=k: p.at(p.around(k), p.l)) for k in p.ks}
-        self.second = {k: message(p.l, k, lambda: p.at(p.z, p.l2)) for k in ks}
-        self.third = {(j, k): message(lines[j], k, lambda: p.at(p.z, p.l3)) for j in range(2) for k in ks}
-        self.lent = {}
-        if lend:
-            keys = [(j, k) for j in range(4) for k in ks if j or k or own]
-            self.lent = {key: message(lines[key[0]], key[1], lambda: p.sibling) for key in keys}
+        over = range(p.nz)
+        self.second = {i: message(0, i, lambda: p.at(p.z, p.l2)) for i in (over if early else (0,))}
+        self.third = {(j, i): message(j, i, lambda: p.at(p.z, p.l3)) for j in range(2) for i in over}
+        self.chains = [Chain(place, links, lambda s, j=j: at(s, lines[j])) for j in range(1 if early else 2)]
+        keys = [(j, i) for j in range(4) for i in over if j or i or own] if lend else []
+        self.lent = {key: message(*key, lambda: p.sibling) for key in keys}
         self.waited = set()
+        self.all = [*self.second.values(), *self.third.values(), *self.lent.values(), *self.chains]
+
+    def wait_sent(self):
+        for message in self.all:
+            message.wait_send()
 
     def hand_over(self, *key):
         if key in self.lent:
             self.lent[key].start()
 
     def start(self):
-        self.hand_over(0, 0)
+        self.chains[0].start()
         self.second[0].start()
         self.third[0, 0].start()
-        for k in self.p.ks:
-            self.first[k].start()
-
-    def from_z(self, k):
-        self.first[k].wait_recv()
-        self.third[0, k].start()
-        self.second[k].start()
-        self.hand_over(0, k)
-
-    def from_second(self, k):
-        self.second[k].wait_recv()
-        self.third[1, k].start()
-        self.hand_over(1, k)
-
-    def from_third(self, j, k):
-        self.third[j, k].wait_recv()
-        self.hand_over(2 + j, k)
+        self.hand_over(0, 0)
+
+    def over_z(self, j, i):
+        self.chains[j].arrive(i)
+        self.third[j, i].start()
+        if self.early:
+            self.second[i].start()
+        self.hand_over(j, i)
+
+    def over_second(self, i):
+        self.second[i].wait_recv()
+        if not self.early:
+            self.chains[1].start()
+        self.third[1, i].start()
+        self.hand_over(1, i)
+
+    def over_third(self, j, i):
+        self.third[j, i].wait_recv()
+        self.hand_over(2 + j, i)
+
+    def lent_own(self):
+        self.waited.add((0, 0))
+        self.lent[0, 0].wait_recv()
 
     def lent_line(self, j):
-        for k in range(self.p.nz):
-            if (j, k) in self.lent and (j, k) not in self.waited:
-                self.waited.add((j, k))
-                self.lent[j, k].wait_recv()
+        for i in range(self.p.nz):
+            if (j, i) in self.lent and (j, i) not in self.waited:
+                self.waited.add((j, i))
+                self.lent[j, i].wait_recv()
 
     def steps(self):
-        ks = self.p.ks
-        out = [functools.partial(self.from_z, k) for k in ks]
-        out += [functools.partial(self.from_second, k) for k in (0, *ks)]
-        out += [functools.partial(self.from_third, j, k) for j in range(2) for k in (0, *ks)]
-        return out
+        part, over = functools.partial, range(self.p.nz)
+        out = [part(self.over_z, j, i) for j in range(len(self.chains)) for i in over[1:]]
+        out += [part(self.over_second, i) for i in self.second]
+        return out + [part(self.over_third, j, i) for j, i in self.third]
+
+
+def two_ways(place, links, buf, lend, own=False, cuts=(None, None)):
+    return [
+        Gather(place, links, buf, lend, own, early=early, cut=cut) for early, cut in zip((True, False), cuts)
+    ]
 
 
 class Scatter:
@@ -199,15 +332,18 @@
         for message in self.m1.values():
             message.start()
 
-    def stage2(self, o):
+    def far(self, o):
         p, zz = self.p, self.p.around(o)
         self.m1[0, o].wait_recv()
         self.add(zz, p.l2, self.got1()[zz, 0])
         self.m2[o].start()
+
+    def near(self, o):
+        p, zz = self.p, self.p.around(o)
         self.m1[1, o].wait_recv()
         self.add(zz, p.l, self.got1()[zz, 1])
 
-    def stage3(self, o):
+    def along(self, o):
         p, zz = self.p, self.p.around(o)
         self.m2[o].wait_recv()
         if o:
@@ -223,19 +359,16 @@
         return total
 
     def steps(self):
-        out = [functools.partial(self.stage2, self.order[0])]
-        for now, before in zip(self.order[1:], self.order):
-            out += [functools.partial(self.stage2, now), functools.partial(self.stage3, before)]
-        return out + [functools.partial(self.stage3, self.order[-1])]
+        return [functools.partial(step, o) for step in (self.far, self.near, self.along) for o in self.order]
 
 
 def layer_kernel(
     nz,
-    tokens, cot, picked, counts, gain_a_r, gain_m_r, router_r, wqkv_h, wout_h, wup_h, wdown_h,
+    tokens_h, cot_h, picked, counts, gain_a_r, gain_m_r, router_r, wqkv_h, wout_h, wup_h, wdown_h,
     pick_o, rows_o, grow_o, res_o, gup_o, gdown_o, small_o,
-    wqkv, wout, wup, wdown, wsem,
+    tokens, cot, wqkv, wout, wup, wdown, wsem,
     gvec, xall, uall, kall, vall, qst, bias, probs, att,
-    dyb, attn_s, resid_s, logit_s, part, got_a, got_m,
+    dy_s, attn_s, resid_s, logit_s, part, got_a, got_m,
     wall, gall, pre_s, act_s, gpre_s, dost, gq, gkv,
     gsib, gu1, gu2, gu3, share, sh1, sh2, sh3, res,
     sm, smz, smy, smx, smw, stage_u, stage_d, osem,
@@ -253,19 +386,111 @@
     nseq = nz * LINES
     total_rows = nseq * rows
     ff = wup.shape[1]
-    ks = place.ks
 
     barrier = pltpu.get_barrier_semaphore()
-    peers = [place.at(place.around(k), l) for k in range(1, nz)]
-    peers += [place.at(z, place.l2), place.at(z, place.l3), place.sibling]
+    peers = [place.at(z, place.l2), place.at(z, place.l3), place.sibling]
     for peer in peers:
         pl.semaphore_signal(barrier, inc=1, device_id=peer, device_id_type=MESH)
+
+    def greet(on):
+        pl.semaphore_signal(barrier, inc=1, device_id=place.at(on, l), device_id_type=MESH)
+
+    pl.when(z + 1 < nz)(lambda: greet(z + 1))
+    pl.when(z > 0)(lambda: greet(z - 1))
     loads = [
         pltpu.make_async_copy(h, v, wsem.at[i])
-        for i, (h, v) in enumerate(((wqkv_h, wqkv), (wout_h, wout), (wup_h, wup), (wdown_h, wdown)))
+        for i, (h, v) in enumerate(
+            ((tokens_h, tokens), (cot_h, cot), (wqkv_h, wqkv), (wout_h, wout), (wup_h, wup), (wdown_h, wdown))
+        )
     ]
-    for load in loads:
+    for load in loads[:2]:
         load.start()
+
+    cuts = (pl.ds(0, EARLY_ROWS), pl.ds(EARLY_ROWS, rows - EARLY_ROWS))
+    gx = two_ways(place, links, lambda: xall.at[c], True, True, cuts)
+    gw = two_ways(place, links, lambda: wall.at[c], True, False, cuts)
+    gg = two_ways(place, links, lambda: gall.at[c], True, True, cuts)
+    scatters = [
+        Scatter(
+            place, links, lambda g=g: share.at[g], lambda g=g: sh1.at[g], lambda g=g: sh2.at[g], lambda g=g: sh3.at[g]
+        )
+        for g in range(2)
+    ]
+    gathers = [two_ways(place, links, lambda g=g: res.at[g], False, False, (0, 1)) for g in range(2)]
+    reduce_u = Scatter(place, links, lambda: xall.at[c], lambda: gu1, lambda: gu2, lambda: gu3)
+    small = {
+        "y": links.message(lambda: (smy.at[0], smy.at[1], place.at(z, place.l2))),
+        "x": links.message(lambda: (smx.at[0], smx.at[1], place.at(z, place.l3))),
+        "w": links.message(lambda: (smw.at[0], smw.at[1], place.sibling)),
+    }
+    for k in range(1, nz):
+        small[k] = links.message(lambda k=k: (sm, smz.at[k - 1], place.at(place.around(k), l)))
+
+    def begin(flows):
+        for flow in flows:
+            flow.start()
+
+    def small_z():
+        for k in range(1, nz):
+            small[k].wait_recv()
+        total = jnp.zeros(sm.shape, F32)
+        for source in range(nz):
+            for k in range(nz):
+                piece = sm[...] if k == 0 else smz[k - 1]
+                total = total + jnp.where(place.around(nz - k) == source, piece, 0.0)
+        smy[0] = total
+        small["y"].start()
+
+    def small_2():
+        small["y"].wait_recv()
+        smx[0] = smy[0] + smy[1]
+        small["x"].start()
+
+    def small_3():
+        small["x"].wait_recv()
+        smw[0] = smx[0] + smx[1]
+        small["w"].start()
+
+    def small_4():
+        small["w"].wait_recv()
+        total = smw[0] + smw[1]
+        small_o[...] = jnp.where(c == 0, total[:, :half], total[:, half:])
+
+    def weights_out(g):
+        res[g, z, l] = scatters[g].total().astype(BF16)
+        begin(gathers[g])
+
+    def tokens_out():
+        grad = reduce_u.total()
+        own = attn_s[pl.ds(0, rows), :]
+        scale = row_scale(own)
+        hat = own * scale
+        lifted = grad * gain_a
+        grad_x = scale * (lifted - hat * jnp.mean(lifted * hat, axis=-1, keepdims=True))
+        at = pl.ds(pl.multiple_of(c * rows, rows), rows)
+        grow_o[...] = grad_x + resid_s[at, :] + logit_s[at, :] * router
+
+    slots, part_ff = stage_u.shape[:2]
+    hb = slots * part_ff
+    blocks = ff // hb
+    tile = total_rows // 2
+    tiles = 2 * total_rows // tile
+    per_block = tiles + 2
+    steps = [step for flows in (gx, gg, gw, *gathers) for flow in flows for step in flow.steps()]
+    steps += [step for scatter in (*scatters, reduce_u) for step in scatter.steps()]
+    steps += [functools.partial(weights_out, g) for g in range(2)]
+    steps += [small_z, small_2, small_3, small_4, tokens_out]
+    left = set(range(len(steps)))
+
+    def pump(kind, j):
+        for i in SCHEDULE[POINTS[kind] + j]:
+            left.remove(i)
+            steps[i]()
+
+    def pump_in(index, kind, among):
+        for j in among:
+            if SCHEDULE[POINTS[kind] + j]:
+                pl.when(index == j)(functools.partial(pump, kind, j))
 
     itself = lax.broadcasted_iota(jnp.int32, (rows, total_rows), 1) == (
         lax.broadcasted_iota(jnp.int32, (rows, total_rows), 0) + place.me * rows
@@ -279,17 +504,19 @@
         lax.broadcasted_iota(jnp.int32, (rows, block), 1).astype(F32) == own_row, 1.0, 0.0
     ).astype(BF16)
     pick_o[...] = pick
+    loads[0].wait()
     xall[c, z, l] = mm(pick, tokens[...]).astype(BF16)
     gvec[c] = jnp.zeros(gvec.shape[1:], F32)
     for i, ref in enumerate((gain_a_r, gain_m_r, router_r)):
         gvec[c, i : i + 1] = ref[...].astype(F32).reshape(1, half)
-    pl.semaphore_wait(barrier, len(peers))
-
-    gx = Gather(place, links, lambda: xall.at[c], True, own=True)
-    gx.start()
+    pl.semaphore_wait(barrier, len(peers) + jnp.where(z + 1 < nz, 1, 0) + jnp.where(z > 0, 1, 0))
+
+    begin(gx)
+    for load in loads[2:]:
+        load.start()
     vec_copy = links.copy(lambda: (gvec.at[c], gvec.at[c], place.sibling))
-    dyb[c] = mm(pick, cot[...]).astype(BF16)
-    dy_copy = links.copy(lambda: (dyb.at[c], dyb.at[c], place.sibling))
+    loads[1].wait()
+    gall[c, z, l] = mm(pick, cot[...]).astype(BF16)
 
     lane = lax.broadcasted_iota(jnp.int32, (2, total_rows), 1)
     stream = lax.broadcasted_iota(jnp.int32, (2, total_rows), 0)
@@ -312,7 +539,7 @@
     vec_copy.wait_recv()
     vectors = jnp.concatenate([gvec[0], gvec[1]], axis=1)
     gain_a, gain_m, router = vectors[0:1], vectors[1:2], vectors[2:3]
-    loads[0].wait()
+    loads[2].wait()
 
     def project(s, line):
         def norm(zz, carry):
@@ -331,28 +558,15 @@
                     ]
 
     def arrive(j):
-        if j == 0:
-            for k in ks:
-                gx.from_z(k)
-        if j == 1:
-            for k in (0, *ks):
-                gx.from_second(k)
-            gx.lent_line(0)
-        if j == 3:
-            gx.lent_line(1)
-        if j == 4:
-            for k in (0, *ks):
-                gx.from_third(0, k)
-        if j == 5:
-            gx.lent_line(2)
-        if j == 6:
-            for k in (0, *ks):
-                gx.from_third(1, k)
-        if j == 7:
-            gx.lent_line(3)
+        pump("x", j)
+        if j % 2:
+            for flow in gx:
+                flow.lent_line(j // 2)
+        if j == COTANGENT_AT:
+            begin(gg)
 
     def take_line(j, carry):
-        for i in (0, 1, 3, 4, 5, 6, 7):
+        for i in range(8):
             pl.when(j == i)(functools.partial(arrive, i))
         mine = lax.rem(j, 2) == 0
         step = lax.div(j, 2)
@@ -364,7 +578,6 @@
         return carry
 
     lax.fori_loop(0, 8, take_line, 0)
-    early = links.used
     low = lax.broadcasted_iota(jnp.int32, (rows, 128), 1) < HD
 
     def stacked(value, s, p):
@@ -390,16 +603,19 @@
         out = mm(prob.astype(BF16), vals)
         at = pl.multiple_of(p * 128, 128)
         att[s, :, pl.ds(at, 128)] = jnp.where(low, out[:rows], out[rows:]).astype(BF16)
+        pump_in(i, "a", range(2 * pairs))
         return carry
 
     lax.fori_loop(0, 2 * pairs, attend, 0)
-    loads[1].wait()
+    loads[3].wait()
     part[...] = mm(att[...].reshape(both, half), wout[...])
     swap = links.copy(lambda: (part, got_a, place.sibling))
     x_both = xall[:, z, l].reshape(both, width).astype(F32)
+    pump("p", 0)
     weight = jax.nn.sigmoid(jnp.sum(x_both * router, axis=-1, keepdims=True))
     lift = weight * own_live
-    dy_copy.wait_recv()
+    for flow in gg:
+        flow.lent_own()
     swap.wait()
     attn = part[...] + got_a[...]
     attn_s[...] = attn
@@ -407,15 +623,8 @@
     resid_s[...] = resid
     w_both = (resid * row_scale(resid) * gain_m).astype(BF16)
     wall[:, z, l] = w_both.reshape(2, rows, width)
-    gw = Gather(place, links, lambda: wall.at[c], True)
-    gw.start()
-    todo = gw.steps()
-
-    def pump(n):
-        for _ in range(min(n, len(todo))):
-            todo.pop(0)()
-
-    for load in loads[2:]:
+    begin(gw)
+    for load in loads[4:]:
         load.wait()
 
     fb = 384
@@ -424,20 +633,16 @@
         pre = mm(w_both, wup[:, cut])
         pre_s[:, cut] = pre
         act_s[:, cut] = gelu_parts(pre)[0].astype(BF16)
-    pump(3)
+    pump("p", 1)
     part[...] = mm(act_s[...], wdown[...])
     swap = links.copy(lambda: (part, got_m, place.sibling))
-    pump(2)
+    pump("p", 2)
     swap.wait()
     branch = attn_s[...] + (part[...] + got_m[...])
     x_both = xall[:, z, l].reshape(both, width).astype(F32)
-    dy_both = dyb[...].reshape(both, width).astype(F32)
+    dy_both = gall[:, z, l].reshape(both, width).astype(F32)
     grad_branch = dy_both * lift
     g_both = grad_branch.astype(BF16)
-    gall[:, z, l] = g_both.reshape(2, rows, width)
-    gg = Gather(place, links, lambda: gall.at[c], True)
-    gg.start()
-    todo += gg.steps()
     attn_s[...] = x_both + lift * branch
     rows_o[...] = attn_s[pl.ds(pl.multiple_of(c * rows, rows), rows), :].astype(BF16)
     grad_logit = (
@@ -446,15 +651,15 @@
     logit_s[...] = grad_logit
     sm[...] = jnp.zeros_like(sm)
     sm[2:3] = jnp.sum(grad_logit * on_core * x_both, axis=0, keepdims=True)
-    pump(2)
+    pump("p", 3)
     for b in range(ff // fb):
         cut = slice(b * fb, (b + 1) * fb)
         grad_act = mm(g_both, wdown[cut, :], NT)
         gpre_s[:, cut] = (gelu_parts(pre_s[:, cut])[1] * grad_act).astype(BF16)
-    pump(2)
+    pump("p", 4)
     part[...] = mm(gpre_s[...], wup[...], NT)
     swap = links.copy(lambda: (part, got_a, place.sibling))
-    pump(2)
+    pump("p", 5)
     swap.wait()
     grad_w = part[...] + got_a[...]
     resid = resid_s[...]
@@ -464,7 +669,7 @@
     lifted = grad_w * gain_m
     grad_resid = scale_m * (lifted - hat * jnp.mean(lifted * hat, axis=-1, keepdims=True))
     resid_s[...] = grad_resid
-    ga_both = (dyb[...].reshape(both, width).astype(F32) * lift + grad_resid).astype(BF16)
+    ga_both = (gall[:, z, l].reshape(both, width).astype(F32) * lift + grad_resid).astype(BF16)
     attended = att[...].reshape(both, half)
     piece = width // nseq
     grad_o = mm(attended, ga_both, TN).astype(BF16)
@@ -478,13 +683,6 @@
         for p in range(pairs):
             dost[s * pairs + p] = stacked(grad_att, s, p)
 
-    scatters = [
-        Scatter(
-            place, links, lambda g=g: share.at[g], lambda g=g: sh1.at[g], lambda g=g: sh2.at[g], lambda g=g: sh3.at[g]
-        )
-        for g in range(2)
-    ]
-
     def attend_back(s, p):
         i = s * pairs + p
         keys = kall[i].reshape(total_rows, 128)
@@ -518,32 +716,34 @@
 
         lax.fori_loop(0, 2, half_of, 0)
 
-    counts_at = [3, 3, 3, 3, 3, 3]
-    queue = [[todo.pop(0) for _ in range(min(n, len(todo)))] for n in counts_at]
-    queue[-1] += todo
-    del todo[:]
-
     def back(i, carry):
         p, s = lax.div(i, 2), lax.rem(i, 2)
         attend_back(s, p)
         pl.when(s == 1)(lambda: share_pair(p))
-        for j, steps in enumerate(queue):
-
-            def go(steps=steps, j=j):
-                for step in steps:
-                    step()
-                if j == 1:
-                    scatters[0].start()
-                if j == 5:
-                    scatters[1].start()
-
-            pl.when(i == j)(go)
+        pl.when(i == 1)(scatters[0].start)
+        pl.when(i == 2 * pairs - 1)(scatters[1].start)
+        pump_in(i, "b", range(2 * pairs))
         return carry
 
     lax.fori_loop(0, 2 * pairs, back, 0)
-    for message in list(links.pending):
-        if message.i < early:
-            message.wait_send()
+    for flow in gx:
+        flow.wait_sent()
+
+    pump("b", 6)
+    for flow in gg:
+        for j in range(LINES):
+            flow.lent_line(j)
+        flow.wait_sent()
+
+    def weigh(i, carry):
+        s, zz = lax.div(i, nz), lax.rem(i, nz)
+        for line in range(LINES):
+            gate = jax.nn.sigmoid(jnp.sum(xall[s, zz, line].astype(F32) * router, axis=-1, keepdims=True))
+            alive = lax.broadcasted_iota(jnp.int32, (rows, 1), 0) < counts[s, zz * LINES + line]
+            gall[s, zz, line] = (gall[s, zz, line].astype(F32) * jnp.where(alive, gate, 0.0)).astype(BF16)
+        return carry
+
+    lax.fori_loop(0, 2 * nz, weigh, 0)
 
     own_gq = jnp.concatenate([gq[p].reshape(both, 128) for p in range(pairs)], axis=1)
     part[...] = mm(own_gq, wqkv[0], NT)
@@ -560,6 +760,7 @@
     def theirs(j, carry):
         zz = place.around(j + 1)
         xall[other, zz] = grad_u(other, zz).astype(BF16).reshape(LINES, rows, width)
+        pump_in(j, "v", range(nz))
         return carry
 
     lax.fori_loop(0, nz, theirs, 0)
@@ -580,6 +781,7 @@
         rows_x = xall[c, zz].astype(F32)
         hat = rows_x * row_scale(rows_x)
         xall[c, zz] = value.astype(BF16)
+        pump_in(j, "u", range(nz))
         return gain_total + jnp.sum(value * hat, axis=(0, 1)).reshape(1, width)
 
     x_own = xall[c, z, l].astype(F32)
@@ -588,107 +790,17 @@
     gain_total = lax.fori_loop(0, nz, ours, gain_total)
     xall[c, z, l] = (xall[c, z, l].astype(F32) + part_of(c)).astype(BF16)
     sm[0:1] = gain_total
-    reduce_u = Scatter(place, links, lambda: xall.at[c], lambda: gu1, lambda: gu2, lambda: gu3)
     reduce_u.start()
-    for j in range(LINES):
-        gw.lent_line(j)
-        gg.lent_line(j)
-
-    small = {
-        "y": links.message(lambda: (smy.at[0], smy.at[1], place.at(z, place.l2))),
-        "x": links.message(lambda: (smx.at[0], smx.at[1], place.at(z, place.l3))),
-        "w": links.message(lambda: (smw.at[0], smw.at[1], place.sibling)),
-    }
     for k in range(1, nz):
-        small[k] = links.copy(
-            lambda k=k: (sm, smz.at[k - 1], place.at(place.around(k), l))
-        )
-
-    def small_z():
-        for k in range(1, nz):
-            small[k].wait_recv()
-        total = jnp.zeros(sm.shape, F32)
-        for source in range(nz):
-            for k in range(nz):
-                piece = sm[...] if k == 0 else smz[k - 1]
-                total = total + jnp.where(place.around(nz - k) == source, piece, 0.0)
-        smy[0] = total
-        small["y"].start()
-
-    def small_2():
-        small["y"].wait_recv()
-        smx[0] = smy[0] + smy[1]
-        small["x"].start()
-
-    def small_3():
-        small["x"].wait_recv()
-        smw[0] = smx[0] + smx[1]
-        small["w"].start()
-
-    def small_4():
-        small["w"].wait_recv()
-        total = smw[0] + smw[1]
-        small_o[...] = jnp.where(c == 0, total[:, :half], total[:, half:])
-
-    gathers = [Gather(place, links, lambda g=g: res.at[g], False) for g in range(2)]
-
-    def weights_out(g):
-        res[g, z, l] = scatters[g].total().astype(BF16)
-        gathers[g].start()
-
-    def tokens_out():
-        grad = reduce_u.total()
-        own = attn_s[pl.ds(0, rows), :]
-        scale = row_scale(own)
-        hat = own * scale
-        lifted = grad * gain_a
-        grad_x = scale * (lifted - hat * jnp.mean(lifted * hat, axis=-1, keepdims=True))
-        at = pl.ds(pl.multiple_of(c * rows, rows), rows)
-        grow_o[...] = grad_x + resid_s[at, :] + logit_s[at, :] * router
-
-    timed = []
-
-    def plan(steps, begin, end):
-        gap = (end - begin) / max(len(steps) - 1, 1)
-        timed.extend((begin + gap * i, step) for i, step in enumerate(steps))
-
-    plan(scatters[0].steps(), -3, -1)
-    plan([functools.partial(weights_out, 0)], -1, -1)
-    plan([small_z], 1, 1)
-    plan(scatters[1].steps(), 0, 4)
-    plan([functools.partial(weights_out, 1)], 4, 4)
-    plan(gathers[0].steps(), 1, 7)
-    plan(reduce_u.steps(), 3, 11)
-    plan(gathers[1].steps(), 6, 14)
-    plan([small_2, small_3, small_4], 5, 11)
-    plan([tokens_out], 12, 12)
-
-    slots, part_ff = stage_u.shape[:2]
-    hb = slots * part_ff
-    blocks = ff // hb
-    tile = total_rows // 2
-    tiles = 2 * total_rows // tile
-    points = (tiles + 2) * blocks
-    spread = [[] for _ in range(points + 1)]
-    for at, step in sorted(timed, key=lambda pair: pair[0]):
-        if at < 0:
-            step()
-        else:
-            spread[min(int(at), points)].append(step)
+        small[k].start()
+    pump("u", nz)
+    for flow in gw:
+        for j in range(LINES):
+            flow.lent_line(j)
 
     def put(b, i, which, stage, out):
         at = pl.ds(pl.multiple_of(b * hb + i * part_ff, part_ff), part_ff)
         return pltpu.make_async_copy(stage.at[i], out.at[at, :], osem.at[which, i])
-
-    def pumps(point, among):
-        for j in among:
-            if spread[j]:
-
-                def go(steps=spread[j]):
-                    for step in steps:
-                        step()
-
-                pl.when(point == j)(go)
 
     def ff_block(b, carry):
         cut = pl.ds(pl.multiple_of(b * hb, hb), hb)
@@ -703,29 +815,28 @@
             grad_pre = (slope * grad_act).astype(BF16)
             for i in range(slots):
                 gkv[i, s, at] = grad_pre[:, part_ff * i : part_ff * (i + 1)]
-            pumps(b * (tiles + 2) + t, [i for i in range(points) if i % (tiles + 2) < tiles])
+            pump_in(b * per_block + t, "h", [j for j in range(per_block * blocks) if j % per_block < tiles])
             return carry
 
         lax.fori_loop(0, tiles, ff_tile, 0)
 
         def flush(which, stage, out, lhs, rhs):
+            value = mm(lhs, rhs[...].reshape(2 * total_rows, width), TN).astype(BF16)
             for i in range(slots):
                 pl.when(b >= 1)(lambda i=i: put(b - 1, i, which, stage, out).wait())
-                stage[i] = mm(lhs(i), rhs[...].reshape(2 * total_rows, width), TN).astype(BF16)
+                stage[i] = value[i * part_ff : (i + 1) * part_ff]
                 put(b, i, which, stage, out).start()
 
-        flush(
-            0, stage_d, gdown_o,
-            lambda i: uall[:, :, :, :, part_ff * i : part_ff * (i + 1)].reshape(2 * total_rows, part_ff), gall,
-        )
-        pumps(b * (tiles + 2) + tiles, range(tiles, points, tiles + 2))
-        flush(1, stage_u, gup_o, lambda i: gkv[i].reshape(2 * total_rows, part_ff), wall)
-        pumps(b * (tiles + 2) + tiles + 1, range(tiles + 1, points, tiles + 2))
+        flush(0, stage_d, gdown_o, uall[:, :, :, :, :hb].reshape(2 * total_rows, hb), gall)
+        pump_in(b * per_block + tiles, "h", range(tiles, per_block * blocks, per_block))
+        slopes = [gkv[i].reshape(2 * total_rows, part_ff) for i in range(slots)]
+        flush(1, stage_u, gup_o, jnp.concatenate(slopes, axis=1), wall)
+        pump_in(b * per_block + tiles + 1, "h", range(tiles + 1, per_block * blocks, per_block))
         return carry
 
     lax.fori_loop(0, blocks, ff_block, 0)
-    for step in spread[points]:
-        step()
+    pump("z", 0)
+    assert not left
     out_copy = pltpu.make_async_copy(res, res_o, osem.at[2, 0])
     out_copy.start()
     for i in range(slots):
@@ -811,11 +922,12 @@
     both = (2 * rows, width)
     part = (2, 3, piece, 128)
     scratch = [
-        vm((3, width, half), BF16), vm((half, width), BF16), vm((width, ff), BF16), vm((ff, width), BF16), dma((4,)),
+        vm((block, width), BF16), vm((block, width), BF16),
+        vm((3, width, half), BF16), vm((half, width), BF16), vm((width, ff), BF16), vm((ff, width), BF16), dma((6,)),
         vm((2, 8, half), F32), vm(wide, BF16), vm(wide, BF16), vm(heads, BF16), vm(heads, BF16),
         vm((2 * pairs, 2 * rows, 128), BF16), vm((2, rows, total_rows), F32),
         vm((2 * pairs, 2 * rows, total_rows), F32), vm((2, rows, half), BF16),
-        vm((2, rows, width), BF16), vm(both, F32), vm(both, F32), vm((2 * rows, 1), F32),
+        vm((8, 128), F32), vm(both, F32), vm(both, F32), vm((2 * rows, 1), F32),
         vm(both, F32), vm(both, F32), vm(both, F32),
         vm(wide, BF16), vm(wide, BF16), vm((2 * rows, ff), F32), vm((2 * rows, ff), BF16), vm((2 * rows, ff), BF16),
         vm((2 * pairs, 2 * rows, 128), BF16), vm((pairs, 2, rows, 128), BF16), vm((pairs, 2, total_rows, 256), BF16),
@@ -843,7 +955,7 @@
             shaped((ff, width), BF16),
             shaped((8, half), F32),
         ),
-        in_specs=[in_vmem] * 3 + [in_smem] + [in_vmem] * 3 + [in_hbm] * 4,
+        in_specs=[in_hbm] * 2 + [in_vmem, in_smem] + [in_vmem] * 3 + [in_hbm] * 4,
         out_specs=(in_vmem, in_vmem, in_vmem, in_hbm, in_hbm, in_hbm, in_vmem),
         scratch_shapes=scratch,
         compiler_params=pltpu.CompilerParams(

time: 180 us -> 152 us (0.84)
  Pallas kernels: 179 us -> 151 us
    pallas_call x1, Pallas kernels: 169 us -> 141 us  [fused_body(): pl.pallas_call(functools.partial(layer_kernel, nz), out_shape=(shaped((ro...]
where the time goes in v3:
time: 152 us
  Pallas kernels  151 us (99%)
    pallas_call x1, Pallas kernels, fused_body(): pl.pallas_call(functools.partial(layer_kernel, nz), out_shape=(shaped((ro...  141 us
    pallas_call x1, Pallas kernels, fused_body(): pl.pallas_call(finish_kernel, out_shape=(shaped((block, width), BF16), sh...  9.64 us

profile of v3, /device:TPU:0, one launch (start us, length us, event | category | flops | bytes accessed | tf_op | source)
XLA Modules:
  0.0 151.8 jit_solution(9510377937945237430)
XLA Ops:
  0.6 141.4 %layer.1 = (bf16[80,320]{1,0:T(8,128)(2,1)}, bf16[80,768]{1,0:T(8,128)(2,1)}, f32[80,768]{1,0:T(8,128)}, bf16[2,4,4,2,3,48,128]{6,5,4,3,2,1,0:T(8,128)(2,1)}, bf...) custom-call(bf16[320,768]{1,0:T(8,128)(2,1)} %bitcast.4, bf16[320,768]{1,0:T(8,128)(2,1)} %bitcast.6, ...), custom_call_target="tpu_custom_call" | custom-call | tf_op jit(solution)/shard_map/layer/pallas_call | solution.py:947
  142.0 9.6 %finish.1 = (bf16[320,768]{1,0:T(8,128)(2,1)}, bf16[320,768]{1,0:T(8,128)(2,1)}, f32[384]{0:T(512)}, f32[384]{0:T(512)}, f32[384]{0:T(512)}, /*index=5*/f32[3,76...) custom-call(bf16[320,768]{1,0:T(8,128)(2,1)} %bitcast.5, bf16[320,768]{1,0:T(8,128)(2,1)} %bitcast.7, ...), custom_call_target="tpu_custom_call" | custom-call | tf_op jit(solution)/shard_map/finish/pallas_call | solution.py:969

commit v4 on v3

--- a/solution.py
+++ b/solution.py
@@ -18,61 +18,61 @@
 COTANGENT_AT = 1
 POINTS = {"x": 0, "a": 8, "p": 14, "b": 20, "v": 27, "u": 31, "h": 36, "z": 54}
 SCHEDULE = (
-    (0, 16, 21, 7, 15, 1, 2, 24, 22, 17, 18),
-    (23, 26, 5, 3),
-    (8, 6, 19, 4, 10, 27, 20),
-    (9, 25),
-    (30,),
-    (33, 45, 51, 37, 11, 31),
-    (28, 13, 52, 14, 29, 12),
+    (3, 0, 21, 1, 15, 22, 16, 2, 18, 7, 17),
+    (),
+    (19, 4, 5, 6, 20, 8),
+    (10, 24, 9, 23, 25),
+    (11, 30, 33, 27),
+    (52, 51, 37, 26, 45),
+    (28, 14, 31, 29, 12, 13),
     (46,),
-    (56, 34, 38, 32, 48),
-    (41, 49, 53),
-    (35, 39),
+    (38, 41, 34),
+    (32, 53),
+    (56, 49, 48, 35),
+    (54,),
+    (47,),
+    (42,),
+    (50, 39, 36),
+    (40, 55),
+    (57, 43),
+    (44,),
+    (58,),
+    (67, 61, 59, 60),
+    (63, 75, 81),
+    (65, 82),
+    (62, 76, 64, 78, 71),
+    (83, 69, 77, 154, 86, 68, 155),
     (),
-    (47,),
-    (36, 40, 42),
-    (50, 57),
-    (54, 55),
-    (43,),
-    (44,),
-    (59,),
-    (60, 63),
-    (82, 75, 58, 67, 61, 81),
-    (64, 83, 71, 68),
-    (62,),
-    (86, 78, 65),
-    (155, 69, 76, 77, 79),
-    (150, 154, 157, 156, 80),
-    (72, 152),
-    (151, 153, 70),
-    (73, 87, 85),
+    (151,),
+    (79, 156, 152),
+    (72, 84),
+    (150, 153, 80, 73, 66),
     (),
-    (66, 84),
     (),
-    (168, 88, 163, 162),
-    (166,),
+    (85, 163, 157, 162, 166, 87),
+    (70, 168),
     (),
-    (167, 169, 158, 164, 159, 89, 165, 74),
-    (160,),
-    (171, 161),
-    (188, 174),
-    (170, 176),
-    (186, 172),
-    (179, 178),
-    (181, 90, 175, 105, 91, 177, 180),
-    (111, 189, 173, 187),
-    (97, 106, 93, 112, 94),
-    (107, 182, 98, 113, 92),
-    (136, 135, 120, 108, 183, 121, 123, 95, 190, 109),
-    (99, 184, 115, 116, 127),
-    (114, 96),
-    (142, 102, 117, 100, 128, 125),
-    (141, 131, 118, 144, 185),
-    (122, 137, 133, 129, 101),
-    (110, 191, 126, 124, 103),
-    (143, 146, 145, 132, 130, 134, 139, 138),
-    (140, 192, 148, 147, 149, 119, 104),
+    (),
+    (74, 164, 159, 89, 165, 158, 88),
+    (188, 169, 160, 161, 167),
+    (170,),
+    (171, 178),
+    (174, 179),
+    (186, 176, 175),
+    (177, 172),
+    (181, 189, 173, 90, 105, 180),
+    (111, 187, 91),
+    (93, 106, 97),
+    (182, 94, 98),
+    (113, 108, 120, 109, 123, 190, 112, 107),
+    (135, 121, 92, 127, 141, 114, 116, 185),
+    (136, 99, 184, 191, 128, 131, 183),
+    (95, 115, 142, 102),
+    (100, 117, 96, 124, 125, 146, 122, 144, 129),
+    (118, 110, 143),
+    (101, 138, 137, 139, 104, 103, 126, 133),
+    (130, 119),
+    (140, 132, 192, 147, 134, 145, 149, 148),
 )
 MESH = pl.DeviceIdType.MESH
 F32 = jnp.float32
@@ -381,8 +381,7 @@
     rows, width = grow_o.shape
     both = 2 * rows
     block = tokens.shape[0]
-    half = wout.shape[0]
-    pairs = half // 128
+    pairs = wout.shape[0] // 128
     nseq = nz * LINES
     total_rows = nseq * rows
     ff = wup.shape[1]
@@ -397,12 +396,11 @@
 
     pl.when(z + 1 < nz)(lambda: greet(z + 1))
     pl.when(z > 0)(lambda: greet(z - 1))
-    loads = [
-        pltpu.make_async_copy(h, v, wsem.at[i])
-        for i, (h, v) in enumerate(
-            ((tokens_h, tokens), (cot_h, cot), (wqkv_h, wqkv), (wout_h, wout), (wup_h, wup), (wdown_h, wdown))
-        )
-    ]
+    half = wout.shape[0]
+    pairs_of = [(tokens_h, tokens), (cot_h, cot)]
+    pairs_of += [(wqkv_h.at[i], wqkv.at[:, i * half : (i + 1) * half]) for i in range(3)]
+    pairs_of += [(wout_h, wout), (wup_h, wup), (wdown_h, wdown)]
+    loads = [pltpu.make_async_copy(h, v, wsem.at[i]) for i, (h, v) in enumerate(pairs_of)]
     for load in loads[:2]:
         load.start()
 
@@ -539,7 +537,8 @@
     vec_copy.wait_recv()
     vectors = jnp.concatenate([gvec[0], gvec[1]], axis=1)
     gain_a, gain_m, router = vectors[0:1], vectors[1:2], vectors[2:3]
-    loads[2].wait()
+    for load in loads[2:5]:
+        load.wait()
 
     def project(s, line):
         def norm(zz, carry):
@@ -549,13 +548,12 @@
 
         lax.fori_loop(0, nz, norm, 0)
         u = jnp.concatenate([uall[s, zz, line] for zz in range(nz)], axis=0)
-        for j, out in ((1, kall), (2, vall)):
-            value = mm(u, wqkv[j]).astype(BF16)
+        value = mm(u, wqkv[:, half:]).astype(BF16)
+        for j, out in enumerate((kall, vall)):
             for p in range(pairs):
+                at = j * half + p * 128
                 for zz in range(nz):
-                    out[s * pairs + p, zz, line] = value[
-                        zz * rows : (zz + 1) * rows, p * 128 : (p + 1) * 128
-                    ]
+                    out[s * pairs + p, zz, line] = value[zz * rows : (zz + 1) * rows, at : at + 128]
 
     def arrive(j):
         pump("x", j)
@@ -586,7 +584,7 @@
         return jnp.concatenate([jnp.where(low, piece, zero), jnp.where(low, zero, piece)], axis=0)
 
     own_u = uall[:, z, l].reshape(both, width)
-    query = mm(own_u, wqkv[0]).astype(BF16) * jnp.asarray(HD ** (-0.5), BF16)
+    query = mm(own_u, wqkv[:, :half]).astype(BF16) * jnp.asarray(HD ** (-0.5), BF16)
     for s in range(2):
         for p in range(pairs):
             qst[s * pairs + p] = stacked(query, s, p)
@@ -607,7 +605,7 @@
         return carry
 
     lax.fori_loop(0, 2 * pairs, attend, 0)
-    loads[3].wait()
+    loads[5].wait()
     part[...] = mm(att[...].reshape(both, half), wout[...])
     swap = links.copy(lambda: (part, got_a, place.sibling))
     x_both = xall[:, z, l].reshape(both, width).astype(F32)
@@ -624,10 +622,10 @@
     w_both = (resid * row_scale(resid) * gain_m).astype(BF16)
     wall[:, z, l] = w_both.reshape(2, rows, width)
     begin(gw)
-    for load in loads[4:]:
+    for load in loads[6:]:
         load.wait()
 
-    fb = 384
+    fb = 512
     for b in range(ff // fb):
         cut = slice(b * fb, (b + 1) * fb)
         pre = mm(w_both, wup[:, cut])
@@ -746,48 +744,45 @@
     lax.fori_loop(0, 2 * nz, weigh, 0)
 
     own_gq = jnp.concatenate([gq[p].reshape(both, 128) for p in range(pairs)], axis=1)
-    part[...] = mm(own_gq, wqkv[0], NT)
-
-    def grad_u(s, zz):
-        at = pl.ds(pl.multiple_of(zz * (LINES * rows), LINES * rows), LINES * rows)
-        gk = jnp.concatenate([gkv[p, s, at, :128] for p in range(pairs)], axis=1)
-        gv = jnp.concatenate([gkv[p, s, at, 128:] for p in range(pairs)], axis=1)
-        return mm(gk, wqkv[1], NT) + mm(gv, wqkv[2], NT)
+    part[...] = mm(own_gq, wqkv[:, :half], NT)
+
+    def grad_u(s, j):
+        size = 2 * LINES * rows
+        at = pl.ds(pl.multiple_of(j * size, size), size)
+        parts = [gkv[p, s, at, cut] for cut in (slice(0, 128), slice(128, 256)) for p in range(pairs)]
+        return mm(jnp.concatenate(parts, axis=1), wqkv[:, half:], NT).reshape(2, LINES, rows, width)
 
     def part_of(s):
         return part[pl.ds(pl.multiple_of(s * rows, rows), rows), :]
 
     def theirs(j, carry):
-        zz = place.around(j + 1)
-        xall[other, zz] = grad_u(other, zz).astype(BF16).reshape(LINES, rows, width)
-        pump_in(j, "v", range(nz))
+        xall[other, pl.ds(2 * j, 2)] = grad_u(other, j).astype(BF16)
+        pump_in(j, "v", range(nz // 2))
         return carry
 
-    lax.fori_loop(0, nz, theirs, 0)
+    lax.fori_loop(0, nz // 2, theirs, 0)
     xall[other, z, l] = (xall[other, z, l].astype(F32) + part_of(other)).astype(BF16)
     lent = [
-        links.copy(
-            lambda j=j: (xall.at[other, place.around(j + 1)], gsib.at[place.around(j + 1)], place.sibling)
-        )
-        for j in range(nz)
+        links.copy(lambda j=j: (xall.at[other, pl.ds(2 * j, 2)], gsib.at[pl.ds(2 * j, 2)], place.sibling))
+        for j in range(nz // 2)
     ]
 
     def ours(j, gain_total):
-        zz = place.around(j + 1)
-        value = grad_u(c, zz).reshape(LINES, rows, width)
-        for i in range(nz):
+        value = grad_u(c, j)
+        for i in range(nz // 2):
             pl.when(j == i)(lent[i].wait_recv)
-        value = value + gsib[zz].astype(F32)
-        rows_x = xall[c, zz].astype(F32)
+        at = pl.ds(2 * j, 2)
+        value = value + gsib[at].astype(F32)
+        rows_x = xall[c, at].astype(F32)
         hat = rows_x * row_scale(rows_x)
-        xall[c, zz] = value.astype(BF16)
-        pump_in(j, "u", range(nz))
-        return gain_total + jnp.sum(value * hat, axis=(0, 1)).reshape(1, width)
+        xall[c, at] = value.astype(BF16)
+        pump_in(j, "u", range(nz // 2))
+        return gain_total + jnp.sum(value * hat, axis=(0, 1, 2)).reshape(1, width)
 
     x_own = xall[c, z, l].astype(F32)
     gain_total = jnp.sum(part_of(c) * (x_own * row_scale(x_own)), axis=0, keepdims=True)
     attn_s[pl.ds(0, rows), :] = x_own
-    gain_total = lax.fori_loop(0, nz, ours, gain_total)
+    gain_total = lax.fori_loop(0, nz // 2, ours, gain_total)
     xall[c, z, l] = (xall[c, z, l].astype(F32) + part_of(c)).astype(BF16)
     sm[0:1] = gain_total
     reduce_u.start()
@@ -820,11 +815,17 @@
 
         lax.fori_loop(0, tiles, ff_tile, 0)
 
+        @pl.when(b >= 1)
+        def _():
+            for i in range(slots):
+                put(b - 1, i, 0, stage_d, gdown_o).wait()
+                put(b - 1, i, 1, stage_u, gup_o).wait()
+
         def flush(which, stage, out, lhs, rhs):
             value = mm(lhs, rhs[...].reshape(2 * total_rows, width), TN).astype(BF16)
             for i in range(slots):
-                pl.when(b >= 1)(lambda i=i: put(b - 1, i, which, stage, out).wait())
                 stage[i] = value[i * part_ff : (i + 1) * part_ff]
+            for i in range(slots):
                 put(b, i, which, stage, out).start()
 
         flush(0, stage_d, gdown_o, uall[:, :, :, :, :hb].reshape(2 * total_rows, hb), gall)
@@ -923,7 +924,7 @@
     part = (2, 3, piece, 128)
     scratch = [
         vm((block, width), BF16), vm((block, width), BF16),
-        vm((3, width, half), BF16), vm((half, width), BF16), vm((width, ff), BF16), vm((ff, width), BF16), dma((6,)),
+        vm((width, 3 * half), BF16), vm((half, width), BF16), vm((width, ff), BF16), vm((ff, width), BF16), dma((8,)),
         vm((2, 8, half), F32), vm(wide, BF16), vm(wide, BF16), vm(heads, BF16), vm(heads, BF16),
         vm((2 * pairs, 2 * rows, 128), BF16), vm((2, rows, total_rows), F32),
         vm((2 * pairs, 2 * rows, total_rows), F32), vm((2, rows, half), BF16),

time: 152 us -> 145 us (0.954)
  Pallas kernels: 151 us -> 144 us
    pallas_call x1, Pallas kernels: 141 us -> 134 us  [fused_body(): pl.pallas_call(functools.partial(layer_kernel, nz), out_shape=(shaped((ro...]
where the time goes in v4:
time: 145 us; the launch traced here: 144 us
  Pallas kernels  144 us (99%)
    pallas_call x1, Pallas kernels, fused_body(): pl.pallas_call(functools.partial(layer_kernel, nz), out_shape=(shaped((ro...  134 us
    pallas_call x1, Pallas kernels, fused_body(): pl.pallas_call(finish_kernel, out_shape=(shaped((block, width), BF16), sh...  9.63 us

profile of v4, /device:TPU:0, one launch (start us, length us, event | category | flops | bytes accessed | tf_op | source)
XLA Modules:
  0.0 144.5 jit_solution(17674838056774357245)
XLA Ops:
  0.6 134.1 %layer.1 = (bf16[80,320]{1,0:T(8,128)(2,1)}, bf16[80,768]{1,0:T(8,128)(2,1)}, f32[80,768]{1,0:T(8,128)}, bf16[2,4,4,2,3,48,128]{6,5,4,3,2,1,0:T(8,128)(2,1)}, bf...) custom-call(bf16[320,768]{1,0:T(8,128)(2,1)} %bitcast.4, bf16[320,768]{1,0:T(8,128)(2,1)} %bitcast.6, ...), custom_call_target="tpu_custom_call" | custom-call | tf_op jit(solution)/shard_map/layer/pallas_call | solution.py:948
  134.7 9.6 %finish.1 = (bf16[320,768]{1,0:T(8,128)(2,1)}, bf16[320,768]{1,0:T(8,128)(2,1)}, f32[384]{0:T(512)}, f32[384]{0:T(512)}, f32[384]{0:T(512)}, /*index=5*/f32[3,76...) custom-call(bf16[320,768]{1,0:T(8,128)(2,1)} %bitcast.5, bf16[320,768]{1,0:T(8,128)(2,1)} %bitcast.7, ...), custom_call_target="tpu_custom_call" | custom-call | tf_op jit(solution)/shard_map/finish/pallas_call | solution.py:970

commit v5 on v4

--- a/solution.py
+++ b/solution.py
@@ -18,61 +18,61 @@
 COTANGENT_AT = 1
 POINTS = {"x": 0, "a": 8, "p": 14, "b": 20, "v": 27, "u": 31, "h": 36, "z": 54}
 SCHEDULE = (
-    (3, 0, 21, 1, 15, 22, 16, 2, 18, 7, 17),
+    (3, 0, 1, 15, 21, 16, 2, 17, 11, 4),
+    (18, 19, 26, 9),
+    (7, 5, 24, 6, 23, 20),
+    (22, 10, 25, 8),
+    (27, 30),
+    (51, 12, 33, 45),
+    (29, 13, 28, 14),
+    (52, 37, 31),
+    (41, 56, 34),
+    (46,),
+    (32, 48),
+    (38, 53),
+    (35, 49),
+    (42,),
+    (39, 47, 54),
+    (36,),
     (),
-    (19, 4, 5, 6, 20, 8),
-    (10, 24, 9, 23, 25),
-    (11, 30, 33, 27),
-    (52, 51, 37, 26, 45),
-    (28, 14, 31, 29, 12, 13),
-    (46,),
-    (38, 41, 34),
-    (32, 53),
-    (56, 49, 48, 35),
-    (54,),
-    (47,),
-    (42,),
-    (50, 39, 36),
-    (40, 55),
-    (57, 43),
-    (44,),
-    (58,),
-    (67, 61, 59, 60),
-    (63, 75, 81),
-    (65, 82),
-    (62, 76, 64, 78, 71),
-    (83, 69, 77, 154, 86, 68, 155),
-    (),
-    (151,),
-    (79, 156, 152),
-    (72, 84),
-    (150, 153, 80, 73, 66),
+    (40, 57),
+    (50, 43, 55),
+    (63, 61, 60, 58),
+    (75, 81, 82, 44),
+    (62, 69, 65),
+    (67, 76, 64, 78, 59, 71, 79),
+    (68, 86, 154, 151),
+    (77, 150),
+    (153, 156, 83),
+    (152,),
+    (80, 157),
+    (88, 66, 70, 73, 155),
     (),
     (),
-    (85, 163, 157, 162, 166, 87),
-    (70, 168),
+    (87, 158),
+    (162, 84, 85, 72),
     (),
     (),
-    (74, 164, 159, 89, 165, 158, 88),
-    (188, 169, 160, 161, 167),
-    (170,),
-    (171, 178),
-    (174, 179),
-    (186, 176, 175),
-    (177, 172),
-    (181, 189, 173, 90, 105, 180),
-    (111, 187, 91),
-    (93, 106, 97),
-    (182, 94, 98),
-    (113, 108, 120, 109, 123, 190, 112, 107),
-    (135, 121, 92, 127, 141, 114, 116, 185),
-    (136, 99, 184, 191, 128, 131, 183),
-    (95, 115, 142, 102),
-    (100, 117, 96, 124, 125, 146, 122, 144, 129),
-    (118, 110, 143),
-    (101, 138, 137, 139, 104, 103, 126, 133),
-    (130, 119),
-    (140, 132, 192, 147, 134, 145, 149, 148),
+    (164, 159, 163, 89, 168, 166, 193, 194, 195, 167, 74, 196),
+    (160, 170, 169, 161),
+    (165, 171, 188, 174),
+    (172,),
+    (175,),
+    (186, 178),
+    (177, 180, 176),
+    (189,),
+    (90, 105, 173, 187, 179),
+    (111, 181, 97),
+    (93, 106, 182, 91, 112),
+    (107, 190, 94, 120, 135, 185, 108, 109),
+    (123, 136, 141, 121, 92, 98, 127),
+    (113, 116, 99, 142),
+    (115, 124, 184, 191, 183),
+    (101, 118, 102, 110, 128, 144, 122),
+    (114, 95, 143, 96, 138, 129),
+    (131, 125, 139, 100, 126, 119),
+    (147, 146, 103),
+    (137, 140, 133, 192, 117, 148, 130, 132, 145, 134, 104, 149),
 )
 MESH = pl.DeviceIdType.MESH
 F32 = jnp.float32
@@ -328,9 +328,13 @@
         acc = self.acc()
         acc[z, line] = (acc[z, line].astype(F32) + got.astype(F32)).astype(BF16)
 
+    def launch(self, o):
+        for j in range(2):
+            self.m1[j, o].start()
+
     def start(self):
-        for message in self.m1.values():
-            message.start()
+        for o in self.order:
+            self.launch(o)
 
     def far(self, o):
         p, zz = self.p, self.p.around(o)
@@ -478,6 +482,7 @@
     steps += [step for scatter in (*scatters, reduce_u) for step in scatter.steps()]
     steps += [functools.partial(weights_out, g) for g in range(2)]
     steps += [small_z, small_2, small_3, small_4, tokens_out]
+    steps += [functools.partial(reduce_u.launch, o) for o in reduce_u.order]
     left = set(range(len(steps)))
 
     def pump(kind, j):
@@ -785,7 +790,6 @@
     gain_total = lax.fori_loop(0, nz // 2, ours, gain_total)
     xall[c, z, l] = (xall[c, z, l].astype(F32) + part_of(c)).astype(BF16)
     sm[0:1] = gain_total
-    reduce_u.start()
     for k in range(1, nz):
         small[k].start()
     pump("u", nz)

time: 145 us -> 143 us (0.986)
  Pallas kernels: 144 us -> 142 us
    pallas_call x1, Pallas kernels: 134 us -> 132 us  [fused_body(): pl.pallas_call(functools.partial(layer_kernel, nz), out_shape=(shaped((ro...]
where the time goes in v5:
time: 143 us
  Pallas kernels  142 us (99%)
    pallas_call x1, Pallas kernels, fused_body(): pl.pallas_call(functools.partial(layer_kernel, nz), out_shape=(shaped((ro...  132 us
    pallas_call x1, Pallas kernels, fused_body(): pl.pallas_call(finish_kernel, out_shape=(shaped((block, width), BF16), sh...  9.63 us

profile of v5, /device:TPU:0, one launch (start us, length us, event | category | flops | bytes accessed | tf_op | source)
XLA Modules:
  0.0 142.8 jit_solution(2076835089992510145)
XLA Ops:
  0.6 132.4 %layer.1 = (bf16[80,320]{1,0:T(8,128)(2,1)}, bf16[80,768]{1,0:T(8,128)(2,1)}, f32[80,768]{1,0:T(8,128)}, bf16[2,4,4,2,3,48,128]{6,5,4,3,2,1,0:T(8,128)(2,1)}, bf...) custom-call(bf16[320,768]{1,0:T(8,128)(2,1)} %bitcast.4, bf16[320,768]{1,0:T(8,128)(2,1)} %bitcast.6, ...), custom_call_target="tpu_custom_call" | custom-call | tf_op jit(solution)/shard_map/layer/pallas_call | solution.py:952
  133.1 9.6 %finish.1 = (bf16[320,768]{1,0:T(8,128)(2,1)}, bf16[320,768]{1,0:T(8,128)(2,1)}, f32[384]{0:T(512)}, f32[384]{0:T(512)}, f32[384]{0:T(512)}, /*index=5*/f32[3,76...) custom-call(bf16[320,768]{1,0:T(8,128)(2,1)} %bitcast.5, bf16[320,768]{1,0:T(8,128)(2,1)} %bitcast.7, ...), custom_call_target="tpu_custom_call" | custom-call | tf_op jit(solution)/shard_map/finish/pallas_call | solution.py:974
